TPU v7x, 128 devices: a whole 4x4x4 slice. The times are simulated.
128 devices in a mesh: gx: 8 (over y, core), gy: 16 (over x, z).
Axes of the slice: x: 4, y: 4, z: 4, core: 2. Of those that a mesh axis runs over, the one named last changes fastest.
Arguments:
- payload: bfloat16 [16384, 4, 35, 128], P(('gx', 'gy')), may hold values from -6 to 6
- opacity: bfloat16 [16384, 4, 128], P(('gx', 'gy')), may hold values from 0.049804688 to 0.34960938
- depth_order: int32 [1024, 16], P(('gx', 'gy')), may hold values from 0 to 127, as said below
- footprints: int32 [128, 128], replicated, may hold values from 0 to 1023, as said below
- panel_map: int32 [16], replicated, may hold values from 0 to 15, each once
- conv1_weight: bfloat16 [9, 32, 36], replicated, may hold values from -0.3125 to 0.3125
- conv1_bias: float32 [32], replicated, may hold values from -3 to 3
- conv2_weight: bfloat16 [9, 32, 32], replicated, may hold values from -0.375 to 0.375
- conv2_bias: float32 [32], replicated, may hold values from -3 to 3
Outputs:
- display: bfloat16 [8, 16, 1, 32, 4096], P('gx', 'gy')
Inputs may be any that keep to these rules, and one draw needn't show every extreme that they name: Each tile lists 16 different bricks; brick b lists tile t in footprints exactly when b appears in row t of depth_order, each tile at most once, 128 tiles a brick. The tiles of the brick of device (x, y) are the 4 consecutive screen tile rows 4x + s .. 4x + s + 3 (modulo 32), for some s from 1 to 3, each with all 32 tile columns; so they belong to devices of gx index x or x + 1 modulo 8, every brick has tiles on both, and every device along gy gets exactly 8 of them. `footprints`: tile numbers as described for depth_order.
All inputs are finite; a program needn't handle non-finite values.
Results may differ from a plain program's by a relative error of at most 0.0052.
Values may be sent and summed in bfloat16 or wider, within the bound.
A program may use at most 64 MiB of HBM per device.

v0:
```python
import jax
import jax.numpy as jnp
from jax import lax
from jax.sharding import PartitionSpec as P

TYD = 4


def with_halo(block, sides, width):
    for axis, dim in sides:
        count = lax.axis_size(axis)
        forward = [(i, i + 1) for i in range(count - 1)]
        backward = [(target, source) for source, target in forward]
        low = lax.ppermute(
            lax.slice_in_dim(block, block.shape[dim] - width, None, axis=dim), axis, forward
        )
        high = lax.ppermute(lax.slice_in_dim(block, 0, width, axis=dim), axis, backward)
        block = jnp.concatenate([low, block, high], axis=dim)
    return block


def shifted(block, axis, distance):
    devices = range(lax.axis_size(axis))
    route = [((i - distance) % len(devices), i) for i in devices]
    return lax.ppermute(block, axis, route)


def conv_valid(padded, kernel):
    height = padded.shape[0] - 2
    span_cols = padded.shape[2] - 2
    total = jnp.zeros((height, kernel.shape[1], span_cols), jnp.float32)
    for row_shift in range(3):
        for col_shift in range(3):
            window = padded[row_shift : row_shift + height, :, col_shift : col_shift + span_cols]
            total = total + jnp.einsum(
                "oc,hcw->how",
                kernel[3 * row_shift + col_shift],
                window,
                preferred_element_type=jnp.float32,
            )
    return total


def rimmed(field):
    return with_halo(field, (("gx", 0), ("gy", 2)), 1)


def shards(
    payload,
    opacity,
    depth_order,
    footprints,
    panel_map,
    conv1_weight,
    conv1_bias,
    conv2_weight,
    conv2_bias,
):
    row_groups = lax.axis_size("gx")
    col_groups = lax.axis_size("gy")
    row_place = lax.axis_index("gx")
    col_place = lax.axis_index("gy")
    self_index = row_place * col_groups + col_place
    fragment_count = payload.shape[0]
    pixel_rows = payload.shape[1]
    channels = payload.shape[2]
    pixel_cols = payload.shape[3]
    local_tiles = depth_order.shape[0]
    depth_count = depth_order.shape[1]
    slot_count = 2 * col_groups * local_tiles
    slot_range = jnp.arange(slot_count, dtype=jnp.int32)
    own_tiles = lax.dynamic_slice_in_dim(footprints, self_index, 1, 0)[0]
    owners = own_tiles // local_tiles
    dest_row = owners // col_groups
    dest_col = owners % col_groups
    part_index = (dest_row - row_place) % row_groups
    send_slot = (dest_col * 2 + part_index) * local_tiles + own_tiles % local_tiles
    placer = (slot_range[:, None] == send_slot[None, :]).astype(jnp.bfloat16)
    fragment = jnp.concatenate([payload, opacity[:, :, None, :]], axis=2)
    outbox = jnp.dot(
        placer, fragment.reshape(fragment_count, -1), preferred_element_type=jnp.float32
    ).astype(jnp.bfloat16)
    outbox = outbox.reshape(col_groups, 2, local_tiles, pixel_rows, channels + 1, pixel_cols)
    crossed = lax.all_to_all(outbox, "gy", split_axis=0, concat_axis=0, tiled=True)
    moved = shifted(crossed[:, 1], "gx", 1)
    inbox = jnp.stack([crossed[:, 0], moved], axis=1)
    source_row = depth_order // col_groups
    source_col = depth_order % col_groups
    source_part = (row_place - source_row) % row_groups
    local_range = jnp.arange(local_tiles, dtype=jnp.int32)
    recv_slot = ((source_col * 2 + source_part) * local_tiles + local_range[:, None]).reshape(-1)
    picker = (recv_slot[:, None] == slot_range[None, :]).astype(jnp.bfloat16)
    gathered = jnp.dot(picker, inbox.reshape(slot_count, -1), preferred_element_type=jnp.float32)
    gathered = gathered.reshape(local_tiles, depth_count, pixel_rows, channels + 1, pixel_cols)
    color = jnp.zeros((local_tiles, pixel_rows, channels, pixel_cols), jnp.float32)
    transmit = jnp.ones((local_tiles, pixel_rows, pixel_cols), jnp.float32)
    for depth_step in range(depth_count):
        color = color + transmit[:, :, None, :] * gathered[:, depth_step, :, :channels, :]
        transmit = transmit * (1.0 - gathered[:, depth_step, :, channels, :])
    composite = jnp.concatenate(
        [color.astype(jnp.bfloat16), (1.0 - transmit).astype(jnp.bfloat16)[:, :, None, :]], axis=2
    )
    tile_cols = local_tiles // TYD
    region = composite.reshape(TYD, tile_cols, pixel_rows, channels + 1, pixel_cols)
    region = region.transpose(0, 2, 3, 1, 4).reshape(
        TYD * pixel_rows, channels + 1, tile_cols * pixel_cols
    )
    band_rows = region.shape[0]
    region_cols = region.shape[2]
    bias_one = conv1_bias[None, :, None]
    bias_two = conv2_bias[None, :, None]
    hidden = jax.nn.silu(conv_valid(rimmed(region), conv1_weight) + bias_one).astype(jnp.bfloat16)
    shaded = conv_valid(rimmed(hidden), conv2_weight)
    feature_count = conv2_weight.shape[1]
    shaded = (shaded + bias_two + region[:, :feature_count, :].astype(jnp.float32)).astype(
        jnp.bfloat16
    )
    strip_rows = band_rows // col_groups
    panel_range = jnp.arange(col_groups, dtype=jnp.int32)
    inverse = jnp.sum(
        jnp.where(panel_map[:, None] == panel_range[None, :], panel_range[:, None], 0), axis=0
    )
    pieces = shaded.reshape(col_groups, strip_rows, feature_count, region_cols)[inverse]
    pieces = pieces.reshape(band_rows, feature_count, region_cols)
    shown = lax.all_to_all(pieces, "gy", split_axis=0, concat_axis=2, tiled=True)
    return shown[None, None]


def solution(mesh):
    return jax.shard_map(
        shards,
        mesh=mesh,
        in_specs=(
            P(("gx", "gy"), None, None, None),
            P(("gx", "gy"), None, None),
            P(("gx", "gy"), None),
            P(),
            P(),
            P(),
            P(),
            P(),
            P(),
        ),
        out_specs=P("gx", "gy", None, None, None),
        check_vma=False,
    )
```

profile of v0, /device:TPU:0, one launch (start us, length us, event | category | flops | bytes accessed | tf_op | source)
XLA Modules:
  0.0 299.8 jit_solution(15930506472480113752)
XLA Ops:
  0.0 8.9 %copy.151 = bf16[128,4,35,128]{0,3,2,1:T(8,128)(2,1)} copy(bf16[128,4,35,128]{3,1,2,0:T(4,128)(2,1)} %param.9) | data formatting | bytes 9175040 | tf_op args[0]
  8.9 1.0 copy.150
  9.9 0.7 fusion.111
  10.7 2.7 pad_maximum_fusion.1
  13.4 2.8 convolution_convert_fusion
  16.2 115.5 %all_to_all.20 = bf16[16,2,8,4,36,128]{5,2,4,3,1,0:T(8,128)(2,1)S(1)} all-to-all(bf16[16,2,8,4,36,128]{5,2,4,3,1,0:T(8,128)(2,1)S(1)} %bitcast.181), channel_id=1, replica_groups=mesh['gx'=8,'gy'=16] {'gy'}, dimensions={0} | all-to-all | bytes 18874368 | tf_op jit(solution)/shard_map/all_to_all | solution.py:84
  131.7 4.2 %fusion.124 = (bf16[16,1,8,4,36,128]{5,2,4,3,1,0:T(8,128)(2,1)}, bf16[16,8,4,36,128]{4,1,3,2,0:T(8,128)(2,1)}) fusion(bf16[16,2,8,4,36,128]{5,2,4,3,1,0:T(8,128)(2,1)S(1)} %all_to_all.20), kind=kLoop, calls=%fused_computation.194 | loop fusion | bytes 18874368 | tf_op jit(solution)/shard_map/slice | solution.py:86
  136.0 0.6 pad_clamp_fusion
  136.7 54.3 %collective-permute-done = bf16[16,8,4,36,128]{4,1,3,2,0:T(8,128)(2,1)} collective-permute-done((bf16[16,8,4,36,128]{4,1,3,2,0:T(8,128)(2,1)}, bf16[16,8,4,36,128]{4,1,3,2,0:T(8,128)(2,1)}, u32[]{:S(2)}, u32[]{:S(2)}) %collective-permute-start) | collective-permute-done | bytes 4718624 | tf_op jit(solution)/shard_map/ppermute | solution.py:25
  191.0 8.3 %pad_maximum_fusion = bf16[16,2,8,4,36,128]{5,2,4,3,1,0:T(8,128)(2,1)} fusion(bf16[16,1,8,4,36,128]{5,2,4,3,1,0:T(8,128)(2,1)} %bitcast.8, bf16[16,1,8,4,36,128]{5,2,4,3,1,0:T(8,128)(2,1)} %get-tuple-element.51), kind=kLoop, calls=%fused_computation.2 | loop fusion | flops 4718592 | bytes 18874368 | tf_op jit(solution)/shard_map/stack | solution.py:86
  199.3 12.6 %copy.153 = bf16[18432,256]{1,0:T(8,128)(2,1)} copy(bf16[18432,256]{0,1:T(8,128)(2,1)} %bitcast.182) | data formatting | bytes 18874368 | tf_op jit(solution)/shard_map/dot_general | solution.py:93
  211.9 5.7 %fusion.55 = f32[8,16,4,36,128]{4,1,3,2,0:T(8,128)S(1)} fusion(bf16[4,36,128,256,1]{3,2,1,0,4:T(8,128)(2,1)} %bitcast.184, s32[8,16]{1,0:T(8,128)S(1)} %fusion.101), kind=kOutput, calls=%fused_computation.80 | convolution fusion | flops 1207992320 | bytes 18874880 | tf_op jit(solution)/shard_map/dot_general | solution.py:93
  217.6 0.8 slice_subtract_fusion.15
  218.4 0.9 slice_subtract_fusion.14
  219.3 8.0 %fusion.123 = (f32[8,1,4,35,128]{4,1,3,2,0:T(1,128)}, f32[8,1,4,35,128]{4,1,3,2,0:T(1,128)S(1)}, f32[8,1,4,35,128]{4,1,3,2,0:T(1,128)S(1)}, f32[8,1,4,35,128]{4,...) fusion(f32[8,16,4,36,128]{4,1,3,2,0:T(8,128)S(1)} %fusion.55), kind=kLoop, calls=%fused_computation.193 | loop fusion | bytes 18350080 | tf_op jit(solution)/shard_map/slice | solution.py:98
  227.3 0.9 fusion.122
  228.5 1.1 copy.154
  229.6 1.1 copy.156
  230.7 1.1 copy.158
  231.8 1.1 copy.160
  232.9 1.1 copy.162
  234.0 1.1 copy.164
  235.1 1.1 copy.166
  236.7 2.7 add_convert_fusion
  239.4 0.4 maximum_bitcast_fusion
  240.2 1.3 collective-permute-start.1
  241.5 1.3 collective-permute-start.2
  243.1 2.1 collective-permute-done.2
  245.3 1.3 collective-permute-start.4
  246.6 4.7 %collective-permute-start.3 = (bf16[18,36,1]{2,1,0:T(8,128)(2,1)S(1)}, bf16[18,36,1]{2,1,0:T(8,128)(2,1)S(1)}, u32[]{:S(2)}, u32[]{:S(2)}) collective-permute-start(bf16[18,36,1]{2,1,0:T(8,128)(2,1)S(1)} %get-tuple-element.53), channel_id=1, source_target_pairs={{0,1},{1,2},{2,3},{3,4},{4,5},{5,6},{6,7},{7,8},{8,9},{9,10},{10,1... | collective-permute-start | bytes 3896 | tf_op jit(solution)/shard_map/ppermute | solution.py:14
  251.8 3.1 %collective-permute-done.3 = bf16[18,36,1]{2,1,0:T(8,128)(2,1)S(1)} collective-permute-done((bf16[18,36,1]{2,1,0:T(8,128)(2,1)S(1)}, bf16[18,36,1]{2,1,0:T(8,128)(2,1)S(1)}, u32[]{:S(2)}, u32[]{:S(2)}) %collective-permute-start.3) | collective-permute-done | bytes 1328 | tf_op jit(solution)/shard_map/ppermute | solution.py:14
  254.9 0.3 fusion.32
  255.2 0.3 fusion.38
  255.5 0.3 fusion.29
  255.9 0.3 fusion.36
  256.2 0.3 fusion.7
  256.6 0.4 multiply_convert_fusion
  257.0 3.3 %collective-permute-start.5 = (bf16[1,32,256]{2,1,0:T(8,128)(2,1)S(1)}, bf16[1,32,256]{2,1,0:T(8,128)(2,1)S(1)}, u32[]{:S(2)}, u32[]{:S(2)}) collective-permute-start(bf16[1,32,256]{2,1,0:T(8,128)(2,1)S(1)} %get-tuple-element.61), channel_id=1, source_target_pairs={{0,16},{16,32},{32,48},{48,64},{64,80},{80,96},{96,112},{1,17},{17... | collective-permute-start | bytes 49160 | tf_op jit(solution)/shard_map/ppermute | solution.py:14
  260.3 1.3 collective-permute-start.6
  261.8 3.0 %collective-permute-done.6 = bf16[1,32,256]{2,1,0:T(8,128)(2,1)S(1)} collective-permute-done((bf16[1,32,256]{2,1,0:T(8,128)(2,1)S(1)}, bf16[1,32,256]{2,1,0:T(8,128)(2,1)S(1)}, u32[]{:S(2)}, u32[]{:S(2)}) %collective-permute-start.6) | collective-permute-done | bytes 16416 | tf_op jit(solution)/shard_map/ppermute | solution.py:17
  265.0 4.4 %collective-permute-start.7 = (bf16[18,32,1]{2,1,0:T(8,128)(2,1)S(1)}, bf16[18,32,1]{2,1,0:T(8,128)(2,1)S(1)}, u32[]{:S(2)}, u32[]{:S(2)}) collective-permute-start(bf16[18,32,1]{2,1,0:T(8,128)(2,1)S(1)} %get-tuple-element.59), channel_id=1, source_target_pairs={{0,1},{1,2},{2,3},{3,4},{4,5},{5,6},{6,7},{7,8},{8,9},{9,10},{10,1... | collective-permute-start | bytes 3464 | tf_op jit(solution)/shard_map/ppermute | solution.py:14
  269.4 1.3 collective-permute-start.8
  271.2 0.9 collective-permute-done.7
  272.1 4.7 %collective-permute-done.8 = bf16[18,32,1]{2,1,0:T(8,128)(2,1)S(1)} collective-permute-done((bf16[18,32,1]{2,1,0:T(8,128)(2,1)S(1)}, bf16[18,32,1]{2,1,0:T(8,128)(2,1)S(1)}, u32[]{:S(2)}, u32[]{:S(2)}) %collective-permute-start.8) | collective-permute-done | bytes 1184 | tf_op jit(solution)/shard_map/ppermute | solution.py:17
  278.3 0.3 fusion.17
  278.7 0.7 gather_fusion
  279.4 19.5 %all_to_all.21 = bf16[16,32,256]{2,1,0:T(8,128)(2,1)S(1)} all-to-all(bf16[16,32,256]{2,1,0:T(8,128)(2,1)S(1)} %gather_fusion), channel_id=1, replica_groups=mesh['gx'=8,'gy'=16] {'gy'}, dimensions={0} | all-to-all | bytes 524288 | tf_op jit(solution)/shard_map/all_to_all | solution.py:125
  299.0 0.8 broadcast_in_dim.15
  (68 shorter events, 4.2 us)
Async XLA Ops:
  131.7 4.2 %copy-start.4 = (s32[16]{0:T(128)S(1)}, s32[16]{0:T(128)}, u32[]{:S(2)}) copy-start(s32[16]{0:T(128)} %param.13) | copy-start | bytes 196
  131.7 4.9 %copy-start.2 = (s32[8,16]{1,0:T(8,128)S(1)}, s32[8,16]{1,0:T(8,128)}, u32[]{:S(2)}) copy-start(s32[8,16]{1,0:T(8,128)} %param.11) | copy-start | bytes 1540
  135.9 55.1 %collective-permute-start = (bf16[16,8,4,36,128]{4,1,3,2,0:T(8,128)(2,1)}, bf16[16,8,4,36,128]{4,1,3,2,0:T(8,128)(2,1)}, u32[]{:S(2)}, u32[]{:S(2)}) collective-permute-start(bf16[16,8,4,36,128]{4,1,3,2,0:T(8,128)(2,1)} %get-tuple-element.52), channel_id=1, source_target_pairs={{112,0},{0,16},{16,32},{32,48},{48,64},{64,80},{80,96},{96,112},{1... | collective-permute-start | bytes 14155784 | tf_op jit(solution)/shard_map/ppermute | solution.py:25
  236.3 6.5 %copy-start.1 = (bf16[9,32,36]{2,1,0:T(8,128)(2,1)S(1)}, bf16[9,32,36]{2,1,0:T(8,128)(2,1)}, u32[]{:S(2)}) copy-start(bf16[9,32,36]{2,1,0:T(8,128)(2,1)} %param.14) | copy-start | bytes 62212
  236.7 19.9 %copy-start.5 = (f32[32]{0:T(128)S(1)}, f32[32]{0:T(128)}, u32[]{:S(2)}) copy-start(f32[32]{0:T(128)} %param.15) | copy-start | bytes 388
  239.4 22.2 %copy-start = (bf16[9,32,32]{2,1,0:T(8,128)(2,1)S(1)}, bf16[9,32,32]{2,1,0:T(8,128)(2,1)}, u32[]{:S(2)}) copy-start(bf16[9,32,32]{2,1,0:T(8,128)(2,1)} %param.16) | copy-start | bytes 55300
  240.2 2.8 collective-permute-start.1
  241.5 3.7 %collective-permute-start.2 = (bf16[1,36,256]{2,1,0:T(8,128)(2,1)S(1)}, bf16[1,36,256]{2,1,0:T(8,128)(2,1)S(1)}, u32[]{:S(2)}, u32[]{:S(2)}) collective-permute-start(bf16[1,36,256]{2,1,0:T(8,128)(2,1)S(1)} %get-tuple-element.55), channel_id=1, source_target_pairs={{16,0},{32,16},{48,32},{64,48},{80,64},{96,80},{112,96},{17,1},{33... | collective-permute-start | bytes 55304 | tf_op jit(solution)/shard_map/ppermute | solution.py:17
  245.3 10.2 %collective-permute-start.4 = (bf16[18,36,1]{2,1,0:T(8,128)(2,1)S(1)}, bf16[18,36,1]{2,1,0:T(8,128)(2,1)S(1)}, u32[]{:S(2)}, u32[]{:S(2)}) collective-permute-start(bf16[18,36,1]{2,1,0:T(8,128)(2,1)S(1)} %get-tuple-element.54), channel_id=1, source_target_pairs={{1,0},{2,1},{3,2},{4,3},{5,4},{6,5},{7,6},{8,7},{9,8},{10,9},{11,1... | collective-permute-start | bytes 3896 | tf_op jit(solution)/shard_map/ppermute | solution.py:17
  246.6 8.3 %collective-permute-start.3 = (bf16[18,36,1]{2,1,0:T(8,128)(2,1)S(1)}, bf16[18,36,1]{2,1,0:T(8,128)(2,1)S(1)}, u32[]{:S(2)}, u32[]{:S(2)}) collective-permute-start(bf16[18,36,1]{2,1,0:T(8,128)(2,1)S(1)} %get-tuple-element.53), channel_id=1, source_target_pairs={{0,1},{1,2},{2,3},{3,4},{4,5},{5,6},{6,7},{7,8},{8,9},{9,10},{10,1... | collective-permute-start | bytes 3896 | tf_op jit(solution)/shard_map/ppermute | solution.py:14
  255.9 22.4 %copy-start.3 = (f32[32]{0:T(128)S(1)}, f32[32]{0:T(128)}, u32[]{:S(2)}) copy-start(f32[32]{0:T(128)} %param.17) | copy-start | bytes 388
  257.0 4.8 %collective-permute-start.5 = (bf16[1,32,256]{2,1,0:T(8,128)(2,1)S(1)}, bf16[1,32,256]{2,1,0:T(8,128)(2,1)S(1)}, u32[]{:S(2)}, u32[]{:S(2)}) collective-permute-start(bf16[1,32,256]{2,1,0:T(8,128)(2,1)S(1)} %get-tuple-element.61), channel_id=1, source_target_pairs={{0,16},{16,32},{32,48},{48,64},{64,80},{80,96},{96,112},{1,17},{17... | collective-permute-start | bytes 49160 | tf_op jit(solution)/shard_map/ppermute | solution.py:14
  260.3 4.6 %collective-permute-start.6 = (bf16[1,32,256]{2,1,0:T(8,128)(2,1)S(1)}, bf16[1,32,256]{2,1,0:T(8,128)(2,1)S(1)}, u32[]{:S(2)}, u32[]{:S(2)}) collective-permute-start(bf16[1,32,256]{2,1,0:T(8,128)(2,1)S(1)} %get-tuple-element.62), channel_id=1, source_target_pairs={{16,0},{32,16},{48,32},{64,48},{80,64},{96,80},{112,96},{17,1},{33... | collective-permute-start | bytes 49160 | tf_op jit(solution)/shard_map/ppermute | solution.py:17
  265.0 7.1 %collective-permute-start.7 = (bf16[18,32,1]{2,1,0:T(8,128)(2,1)S(1)}, bf16[18,32,1]{2,1,0:T(8,128)(2,1)S(1)}, u32[]{:S(2)}, u32[]{:S(2)}) collective-permute-start(bf16[18,32,1]{2,1,0:T(8,128)(2,1)S(1)} %get-tuple-element.59), channel_id=1, source_target_pairs={{0,1},{1,2},{2,3},{3,4},{4,5},{5,6},{6,7},{7,8},{8,9},{9,10},{10,1... | collective-permute-start | bytes 3464 | tf_op jit(solution)/shard_map/ppermute | solution.py:14
  269.4 7.4 %collective-permute-start.8 = (bf16[18,32,1]{2,1,0:T(8,128)(2,1)S(1)}, bf16[18,32,1]{2,1,0:T(8,128)(2,1)S(1)}, u32[]{:S(2)}, u32[]{:S(2)}) collective-permute-start(bf16[18,32,1]{2,1,0:T(8,128)(2,1)S(1)} %get-tuple-element.60), channel_id=1, source_target_pairs={{1,0},{2,1},{3,2},{4,3},{5,4},{6,5},{7,6},{8,7},{9,8},{10,9},{11,1... | collective-permute-start | bytes 3464 | tf_op jit(solution)/shard_map/ppermute | solution.py:17
where the time goes:
time: 302 us; the launch traced here: 300 us
  blocking collectives  135 us (45%)
  waiting for transfers between devices  68.3 us (23%)
  local copies, waits for them, and re-layouts  45.3 us (15%)
  starting transfers between devices  18.9 us (6%)
  other arithmetic  18.4 us (6%)
  matrix products  13.3 us (4%)
    all_to_all x1, blocking collectives, shards(): lax.all_to_all(outbox, 'gy', split_axis=0, concat_axis=0, tiled=True)  116 us
    ppermute x1, waiting for transfers between devices, shifted(): return lax.ppermute(block, axis, route)  54.3 us
    all_to_all x1, blocking collectives, shards(): lax.all_to_all(pieces, 'gy', split_axis=0, concat_axis=2, tiled=True)  19.5 us
    slice x17, local copies, waits for them, and re-layouts, shards(): gathered[:, depth_step, :, :channels, :]  16.1 us
    ppermute x4, starting transfers between devices, with_halo(): lax.ppermute(lax.slice_in_dim(block, block.shape[dim] - width, None, axis...  13.7 us
    dot_general x1, local copies, waits for them, and re-layouts, shards(): jnp.dot(picker, inbox.reshape(slot_count, -1), preferred_element_type=jnp...  12.6 us
    unnamed x16, local copies, waits for them, and re-layouts  10 us
    ppermute x4, waiting for transfers between devices, with_halo(): lax.ppermute(lax.slice_in_dim(block, 0, width, axis=dim), axis, backward)  9.9 us
  transfers between devices with their start and end apart: 9, of which 6 were waited for; matrix products, arithmetic and copies ran while one was open for 1% of the time, Pallas kernels for 0%

commit v1 on v0

v1 whole, which is shorter than its diff:
```python
import functools

import jax
import jax.numpy as jnp
import numpy as np
from jax import lax
from jax.experimental import pallas as pl
from jax.experimental.pallas import tpu as pltpu
from jax.sharding import PartitionSpec as P

MESH = pl.DeviceIdType.MESH
TYD = 4
TXD = 2
TILES = 8
DEPTH = 16
CH = 35
ROWS = 4
COLS = 128
NX = 8
NY = 16
SIDE = 4
TSTEP = DEPTH + 2
MASKS = ((4, 12, 1, 3), (12, 4, 3, 1), (1, 3, 4, 12), (3, 1, 12, 4))


def kappa(q, k):
    m = MASKS[q]
    return (m[1] if k & 4 else 0) ^ (m[2] if k & 2 else 0) ^ (m[3] if k & 1 else 0)


def flip4(p, d):
    if d == 0:
        return p
    if d == 1:
        return p + 1 - 2 * (p % 2)
    if d == 2:
        return (p + 2) % SIDE
    return 3 - p


def paired(c, mask):
    return flip4(c // SIDE, mask // SIDE) * SIDE + flip4(c % SIDE, mask % SIDE)


def tables(footprints, depth_order, gx, gy):
    own = lax.dynamic_slice_in_dim(footprints, gx * NY + gy, 1, 0)[0]
    local = own % TILES
    slot = (own // TILES) % NY * TILES + local
    base = np.zeros((2, 4, 8, 2), np.int32)
    rest = np.zeros((2, 4, 8, 2), np.int32)
    for role in range(2):
        for q in range(4):
            for k in range(8):
                for f in range(2):
                    j, g = q % 2, q // 2
                    jy = (1 + g) if f else (3 if g else 0)
                    base[role, q, k, f] = kappa(q, k) ^ (MASKS[q][0] if role else 0)
                    rest[role, q, k, f] = jy * TXD + j
    owner = jnp.bitwise_xor(jnp.asarray(base.reshape(-1)), gy)
    target = jnp.concatenate(
        [jnp.arange(128, dtype=jnp.int32), owner * TILES + jnp.asarray(rest.reshape(-1))]
    )
    order = jnp.arange(128, dtype=jnp.int32)
    pos = jnp.sum(jnp.where(target[:, None] == slot[None, :], order[None, :], 0), axis=1)

    tile = np.arange(TILES, dtype=np.int32)[:, None]
    part = (gx - depth_order // NY) % NX
    source = (part * NY + depth_order % NY) * 6 + (tile // TXD - 1 + part) * TXD + tile % TXD

    mask = np.zeros((4, 8, 3, 2), np.int32)
    back = np.zeros((4, 8, 3, 2), np.int32)
    which = np.zeros((4, 8, 3, 2), np.int32)
    for q in range(4):
        for k in range(8):
            for e in range(3):
                for s in range(2):
                    j, g = q % 2, q // 2
                    jy = (1 + g) if e != 1 else (3 if g else 0)
                    back[q, k, e, s] = (0, 1 - g, 1)[e]
                    mask[q, k, e, s] = kappa(q, k) ^ (MASKS[q][0] if s else 0)
                    which[q, k, e, s] = jy * TXD + j
    brick = (gx - jnp.asarray(back.reshape(-1))) % NX * NY + jnp.bitwise_xor(
        jnp.asarray(mask.reshape(-1)), gy
    )
    which = jnp.asarray(which.reshape(-1))
    listed = (depth_order + 128 * tile).reshape(-1)
    steps = jnp.tile(jnp.arange(DEPTH, dtype=jnp.int32), TILES)
    hit = (brick + 128 * which)[:, None] == listed[None, :]
    depth = jnp.sum(jnp.where(hit, steps[None, :] - (DEPTH + 1), 0), axis=1) + DEPTH + 1
    return jnp.concatenate([pos, source.reshape(-1), which * TSTEP + depth])


POS_A = 0
POS_K = 128
POS_S = 192
SRC = 256
RET = 384


def reduce_kernel(
    tab, pay_h, opa_h, comp, cov,
    pay, opa, asend, abuf, tb, tsend, trecv, s1, r1, s2, acc, r2, s3, r3, s4, r4, ys, yr,
    lsem, a_s, a_r, t_s, t_r, m_s, m_r, y_s, y_r,
):
    gx = lax.axis_index("gx")
    me = lax.axis_index("gy")
    up = (gx + 1) % NX
    down = (gx + NX - 1) % NX
    loads = [pltpu.make_async_copy(opa_h, opa, lsem.at[4])]
    for i in range(4):
        part = pl.ds(32 * i, 32)
        loads.append(pltpu.make_async_copy(pay_h.at[part], pay.at[part], lsem.at[i]))
    for load in loads:
        load.start()

    barrier = pltpu.get_barrier_semaphore()

    def greet_row(i, _):
        pl.semaphore_signal(barrier, inc=1, device_id=(gx, (me + i) % NY), device_id_type=MESH)
        return 0

    def greet_next(i, _):
        pl.semaphore_signal(barrier, inc=1, device_id=(up, i), device_id_type=MESH)
        pl.semaphore_signal(barrier, inc=1, device_id=(down, i), device_id_type=MESH)
        return 0

    lax.fori_loop(1, NY, greet_row, 0)
    lax.fori_loop(0, NY, greet_next, 0)

    loads[0].wait()

    def pack_alpha(i, _):
        asend[i] = opa[tab[POS_A + i]]
        return 0

    lax.fori_loop(0, 128, pack_alpha, 0, unroll=8)
    for e in range(6):
        abuf[me * 6 + e] = asend[me * TILES + 2 + e]
    pl.semaphore_wait(barrier, 47)

    def alpha_copy(i, back):
        return pltpu.make_async_remote_copy(
            src_ref=asend.at[pl.ds(i * TILES + 2 - 2 * back, 6)],
            dst_ref=abuf.at[pl.ds((back * NY + me) * 6, 6)],
            send_sem=a_s.at[back * NY + i],
            recv_sem=a_r.at[back * NY + me],
            device_id=(up if back else gx, i),
            device_id_type=MESH,
        )

    def alpha_start(n, _):
        alpha_copy((me + n) % NY, 0).start()
        alpha_copy((me + n) % NY, 1).start()
        return 0

    lax.fori_loop(1, NY, alpha_start, 0)
    alpha_copy(me, 1).start()

    for load in loads[1:]:
        load.wait()

    def pack_raw(q, lo, hi):
        def body(k, _):
            for f in range(2):
                s1[q, k, f] = pay[tab[POS_S + (q * 8 + k) * 2 + f]]
            return 0

        lax.fori_loop(lo, hi, body, 0)

    groups = ((4, 8), (2, 4), (1, 2), (0, 1))

    def raw_copy(q, n):
        lo, hi = groups[n]
        part = pl.ds(lo, hi - lo)
        return pltpu.make_async_remote_copy(
            src_ref=s1.at[q, part],
            dst_ref=r1.at[q, part],
            send_sem=m_s.at[q, n],
            recv_sem=m_r.at[q, n],
            device_id=(gx, paired(me, MASKS[q][0])),
            device_id_type=MESH,
        )

    raw = [[raw_copy(q, n) for n in range(4)] for q in range(4)]
    for q in range(4):
        pack_raw(q, 4, 8)
        raw[q][0].start()
    for q in range(4):
        pack_raw(q, 0, 4)

    def alpha_wait(n, _):
        col = (me + n) % NY
        for back in range(2):
            pltpu.make_async_remote_copy(
                src_ref=asend.at[pl.ds(0, 6)],
                dst_ref=abuf.at[pl.ds((back * NY + col) * 6, 6)],
                send_sem=a_s.at[back * NY + col],
                recv_sem=a_r.at[back * NY + col],
                device_id=(gx, col),
                device_id_type=MESH,
            ).wait_recv()
        return 0

    lax.fori_loop(1, NY, alpha_wait, 0)
    alpha_copy(me, 1).wait_recv()

    for t in range(TILES):
        tb[t * TSTEP + DEPTH + 1] = jnp.zeros((ROWS, COLS), jnp.float32)

    def through(d, passed):
        out = []
        for t in range(TILES):
            tb[t * TSTEP + d] = passed[t]
            alpha = abuf[tab[SRC + t * DEPTH + d]].astype(jnp.float32)
            out.append(passed[t] * (1.0 - alpha))
        return tuple(out)

    last = lax.fori_loop(
        0, DEPTH, through, tuple(jnp.ones((ROWS, COLS), jnp.float32) for _ in range(TILES))
    )
    for t in range(TILES):
        cov[t] = (1.0 - last[t]).astype(jnp.bfloat16)

    def fill(i, _):
        tsend[i] = tb[tab[RET + i]]
        return 0

    lax.fori_loop(0, 192, fill, 0, unroll=8)

    def weight_range(q, k, back):
        g = q // 2
        start, size = ((0, 4 if g else 2), (4 if g else 2, 2 if g else 4))[back]
        return pl.ds((q * 8 + k) * 6 + start, size)

    def weight_copy(q, k, back):
        part = weight_range(q, k, back)
        return pltpu.make_async_remote_copy(
            src_ref=tsend.at[part],
            dst_ref=trecv.at[part],
            send_sem=t_s.at[q, k, back],
            recv_sem=t_r.at[q, k, back],
            device_id=(down if back else gx, paired(me, kappa(q, k))),
            device_id_type=MESH,
        )

    weights = {}
    for k in (7, 6, 5, 4, 3, 2, 1, 0):
        for q in range(4):
            for back in range(2):
                if k == 0 and back == 0:
                    g = q // 2
                    for e in range(4 if g else 2):
                        trecv[q * 48 + e] = tsend[q * 48 + e]
                else:
                    weights[q, k, back] = weight_copy(q, k, back)
                    weights[q, k, back].start()
    for q in range(4):
        for n in range(1, 4):
            raw[q][n].start()

    def weighed(q, k):
        own = (q * 8 + k) * 2
        lead = (q * 8 + k) * 6
        own_f = pay[tab[POS_K + own]].astype(jnp.float32)
        got_f = r1[q, k, 0].astype(jnp.float32)
        mid = trecv[lead + 2][None] * own_f + trecv[lead + 3][None] * got_f
        own_a = pay[tab[POS_K + own + 1]].astype(jnp.float32)
        got_a = r1[q, k, 1].astype(jnp.float32)
        first = trecv[lead][None] * own_a + trecv[lead + 1][None] * got_a
        third = trecv[lead + 4][None] * own_a + trecv[lead + 5][None] * got_a
        return first, mid, third

    def merge_sent(q, lo, hi):
        def body(k, _):
            for e, v in enumerate(weighed(q, k)):
                s2[q, k - 4, e] = v.astype(jnp.bfloat16)
            return 0

        lax.fori_loop(lo, hi, body, 0)

    def merge_kept(q, lo, hi):
        def body(k, _):
            for e, v in enumerate(weighed(q, k)):
                acc[q, k, e] = v
            return 0

        lax.fori_loop(lo, hi, body, 0)

    def step_copy(src, dst, q, lo, hi, step, sem):
        part = pl.ds(lo, hi - lo)
        return pltpu.make_async_remote_copy(
            src_ref=src.at[q, part],
            dst_ref=dst.at[q, part],
            send_sem=m_s.at[q, sem],
            recv_sem=m_r.at[q, sem],
            device_id=(gx, paired(me, MASKS[q][step - 1])),
            device_id_type=MESH,
        )

    def wait_weights(q, lo, hi):
        for k in range(lo, hi):
            for back in range(2):
                if (q, k, back) in weights:
                    weights[q, k, back].wait_recv()

    two = [[step_copy(s2, r2, q, lo, hi, 2, 4 + n) for n, (lo, hi) in enumerate(groups[1:])] for q in range(4)]
    three = [[step_copy(s3, r3, q, lo, hi, 3, 7 + n) for n, (lo, hi) in enumerate(groups[2:])] for q in range(4)]
    four = [step_copy(s4, r4, q, 0, 1, 4, 9) for q in range(4)]

    for q in range(4):
        wait_weights(q, 4, 8)
        raw[q][0].wait_recv()
        merge_sent(q, 6, 8)
        two[q][0].start()
    for q in range(4):
        merge_sent(q, 4, 6)
        two[q][1].start()
        two[q][2].start()
    for q in range(4):
        wait_weights(q, 0, 4)
        for n in range(1, 4):
            raw[q][n].wait_recv()
        merge_kept(q, 0, 4)

    def added(src, q, k):
        return [acc[q, k, e] + src[q, k, e].astype(jnp.float32) for e in range(3)]

    def forward(dst, src, q, k, to):
        for e, v in enumerate(added(src, q, k)):
            dst[q, to, e] = v.astype(jnp.bfloat16)

    def keep(src, q, k):
        for e, v in enumerate(added(src, q, k)):
            acc[q, k, e] = v

    for q in range(4):
        two[q][0].wait_recv()
        forward(s3, r2, q, 3, 1)
        three[q][0].start()
        forward(s3, r2, q, 2, 0)
        three[q][1].start()
    for q in range(4):
        two[q][1].wait_recv()
        keep(r2, q, 1)
        two[q][2].wait_recv()
        keep(r2, q, 0)
    for q in range(4):
        three[q][0].wait_recv()
        forward(s4, r3, q, 1, 0)
        four[q].start()
    for q in range(4):
        three[q][1].wait_recv()
        keep(r3, q, 0)

    def cross_copy(q):
        part = pl.ds(q // 2, 2 - q // 2)
        return pltpu.make_async_remote_copy(
            src_ref=ys.at[q, part],
            dst_ref=yr.at[q, part],
            send_sem=y_s.at[q],
            recv_sem=y_r.at[q],
            device_id=(up, me),
            device_id_type=MESH,
        )

    cross = [cross_copy(q) for q in range(4)]
    for q in range(4):
        g, j = q // 2, q % 2
        four[q].wait_recv()
        first, mid, third = added(r4, q, 0)
        ys[q, 1] = third.astype(jnp.bfloat16)
        if g == 0:
            ys[q, 0] = mid.astype(jnp.bfloat16)
        else:
            comp[3 * TXD + j] = mid.astype(jnp.bfloat16)
        cross[q].start()
        acc[q, 0, 0] = first
    for q in range(4):
        g, j = q // 2, q % 2
        cross[q].wait_recv()
        comp[(1 + g) * TXD + j] = (acc[q, 0, 0] + yr[q, 1].astype(jnp.float32)).astype(jnp.bfloat16)
        if g == 0:
            comp[j] = yr[q, 0]

    def alpha_sent(n, _):
        alpha_copy((me + n) % NY, 0).wait_send()
        alpha_copy((me + n) % NY, 1).wait_send()
        return 0

    lax.fori_loop(1, NY, alpha_sent, 0)
    alpha_copy(me, 1).wait_send()
    for copy in weights.values():
        copy.wait_send()
    for q in range(4):
        for copy in raw[q] + two[q] + three[q] + [four[q], cross[q]]:
            copy.wait_send()


def reduce_fragments(tab, payload, opacity):
    unit = (CH, ROWS, COLS)
    bf16, f32 = jnp.bfloat16, jnp.float32
    vmem = pltpu.VMEM
    dma = pltpu.SemaphoreType.DMA
    return pl.pallas_call(
        reduce_kernel,
        name="reduce_fragments",
        out_shape=(
            jax.ShapeDtypeStruct((TILES,) + unit, bf16),
            jax.ShapeDtypeStruct((TILES, ROWS, COLS), bf16),
        ),
        in_specs=[
            pl.BlockSpec(memory_space=pltpu.SMEM),
            pl.BlockSpec(memory_space=pl.ANY),
            pl.BlockSpec(memory_space=pl.ANY),
        ],
        out_specs=(pl.BlockSpec(memory_space=vmem), pl.BlockSpec(memory_space=vmem)),
        scratch_shapes=[
            vmem((128,) + unit, bf16),
            vmem((128, ROWS, COLS), bf16),
            vmem((128, ROWS, COLS), bf16),
            vmem((192, ROWS, COLS), bf16),
            vmem((TILES * TSTEP, ROWS, COLS), f32),
            vmem((192, ROWS, COLS), f32),
            vmem((192, ROWS, COLS), f32),
            vmem((4, 8, 2) + unit, bf16),
            vmem((4, 8, 2) + unit, bf16),
            vmem((4, 4, 3) + unit, bf16),
            vmem((4, 4, 3) + unit, f32),
            vmem((4, 4, 3) + unit, bf16),
            vmem((4, 2, 3) + unit, bf16),
            vmem((4, 2, 3) + unit, bf16),
            vmem((4, 1, 3) + unit, bf16),
            vmem((4, 1, 3) + unit, bf16),
            vmem((4, 2) + unit, bf16),
            vmem((4, 2) + unit, bf16),
            dma((5,)),
            dma((32,)),
            dma((32,)),
            dma((4, 8, 2)),
            dma((4, 8, 2)),
            dma((4, 10)),
            dma((4, 10)),
            dma((4,)),
            dma((4,)),
        ],
        compiler_params=pltpu.CompilerParams(
            collective_id=0, has_side_effects=True, vmem_limit_bytes=48 << 20
        ),
    )(tab, payload, opacity)


def with_halo(block, sides, width):
    for axis, dim in sides:
        count = lax.axis_size(axis)
        forward = [(i, i + 1) for i in range(count - 1)]
        backward = [(target, source) for source, target in forward]
        low = lax.ppermute(
            lax.slice_in_dim(block, block.shape[dim] - width, None, axis=dim), axis, forward
        )
        high = lax.ppermute(lax.slice_in_dim(block, 0, width, axis=dim), axis, backward)
        block = jnp.concatenate([low, block, high], axis=dim)
    return block


def conv_valid(padded, kernel):
    height = padded.shape[0] - 2
    span_cols = padded.shape[2] - 2
    total = jnp.zeros((height, kernel.shape[1], span_cols), jnp.float32)
    for row_shift in range(3):
        for col_shift in range(3):
            window = padded[row_shift : row_shift + height, :, col_shift : col_shift + span_cols]
            total = total + jnp.einsum(
                "oc,hcw->how",
                kernel[3 * row_shift + col_shift],
                window,
                preferred_element_type=jnp.float32,
            )
    return total


def rimmed(field):
    return with_halo(field, (("gx", 0), ("gy", 2)), 1)


def composited(payload, opacity, depth_order, footprints):
    gx = lax.axis_index("gx")
    gy = lax.axis_index("gy")
    tab = tables(footprints, depth_order, gx, gy)
    color, cover = reduce_fragments(tab, payload.transpose(0, 2, 1, 3), opacity)
    composite = jnp.concatenate([color, cover[:, None]], axis=1)
    region = composite.reshape(TYD, TXD, CH + 1, ROWS, COLS).transpose(0, 3, 2, 1, 4)
    return region.reshape(TYD * ROWS, CH + 1, TXD * COLS)


def shards(
    payload, opacity, depth_order, footprints, panel_map,
    conv1_weight, conv1_bias, conv2_weight, conv2_bias,
):
    col_groups = lax.axis_size("gy")
    region = composited(payload, opacity, depth_order, footprints)
    band_rows = region.shape[0]
    region_cols = region.shape[2]
    bias_one = conv1_bias[None, :, None]
    bias_two = conv2_bias[None, :, None]
    hidden = jax.nn.silu(conv_valid(rimmed(region), conv1_weight) + bias_one).astype(jnp.bfloat16)
    shaded = conv_valid(rimmed(hidden), conv2_weight)
    feature_count = conv2_weight.shape[1]
    shaded = (shaded + bias_two + region[:, :feature_count, :].astype(jnp.float32)).astype(
        jnp.bfloat16
    )
    strip_rows = band_rows // col_groups
    panel_range = jnp.arange(col_groups, dtype=jnp.int32)
    inverse = jnp.sum(
        jnp.where(panel_map[:, None] == panel_range[None, :], panel_range[:, None], 0), axis=0
    )
    pieces = shaded.reshape(col_groups, strip_rows, feature_count, region_cols)[inverse]
    pieces = pieces.reshape(band_rows, feature_count, region_cols)
    shown = lax.all_to_all(pieces, "gy", split_axis=0, concat_axis=2, tiled=True)
    return shown[None, None]


SPECS = (
    P(("gx", "gy"), None, None, None),
    P(("gx", "gy"), None, None),
    P(("gx", "gy"), None),
    P(),
    P(),
    P(),
    P(),
    P(),
    P(),
)


def solution(mesh):
    return jax.shard_map(
        shards,
        mesh=mesh,
        in_specs=SPECS,
        out_specs=P("gx", "gy", None, None, None),
        check_vma=False,
    )
```

time: 302 us -> 123 us (0.41)
  blocking collectives: 135 us -> 22 us
  waiting for transfers between devices: 68.3 us -> 12.7 us
  Pallas kernels: 0 us -> 52.9 us
  local copies, waits for them, and re-layouts: 45.3 us -> 5.88 us
  other arithmetic: 18.4 us -> 4.79 us
  matrix products: 13.3 us -> 4.88 us
    all_to_all x1 -> x0, blocking collectives: 116 us -> none  [shards(): lax.all_to_all(outbox, 'gy', split_axis=0, concat_axis=0, tiled=True)]
    ppermute x1 -> x0, waiting for transfers between devices: 54.3 us -> none  [shifted(): return lax.ppermute(block, axis, route)]
    pallas_call x0 -> x1, Pallas kernels: none -> 52.9 us  [reduce_fragments(): pl.pallas_call(reduce_kernel, name='reduce_fragments', out_shape=(jax.Sha...]
    slice x18 -> x0, local copies, waits for them, and re-layouts: 20.3 us -> none  [the longest x17 16.1 us: shards(): gathered[:, depth_step, :, :channels, :]]
    dot_general x1 -> x0, local copies, waits for them, and re-layouts: 12.6 us -> none  [shards(): jnp.dot(picker, inbox.reshape(slot_count, -1), preferred_element_type=jnp...]
    dot_general x2 -> x0, matrix products: 8.5 us -> none  [the longest x1 5.68 us: shards(): jnp.dot(picker, inbox.reshape(slot_count, -1), preferred_element_type=jnp...]
    another operation x1 -> x0, other arithmetic: 8.32 us -> none  [shards(): inbox = jnp.stack([crossed[:, 0], moved], axis=1)]
    unnamed x16, local copies, waits for them, and re-layouts: 10 us -> 3.32 us
  transfers between devices with their start and end apart: 9 -> 8, of which waited for: 6 -> 5; matrix products, arithmetic and copies ran while one was open for 1% -> 2% of each run, Pallas kernels for 0% -> 0%
where the time goes in v1:
time: 123 us; the launch traced here: 121 us
  Pallas kernels  52.9 us (43%)
  blocking collectives  22 us (18%)
  starting transfers between devices  17.9 us (15%)
  waiting for transfers between devices  12.7 us (10%)
  local copies, waits for them, and re-layouts  5.88 us (5%)
  matrix products  4.88 us (4%)
  other arithmetic  4.79 us (4%)
    pallas_call x1, Pallas kernels, reduce_fragments(): pl.pallas_call(reduce_kernel, name='reduce_fragments', out_shape=(jax.Sha...  52.9 us
    all_to_all x1, blocking collectives, shards(): lax.all_to_all(pieces, 'gy', split_axis=0, concat_axis=2, tiled=True)  22 us
    ppermute x4, starting transfers between devices, with_halo(): lax.ppermute(lax.slice_in_dim(block, block.shape[dim] - width, None, axis...  12.7 us
    ppermute x4, waiting for transfers between devices, with_halo(): lax.ppermute(lax.slice_in_dim(block, 0, width, axis=dim), axis, backward)  7.72 us
    ppermute x4, starting transfers between devices, with_halo(): lax.ppermute(lax.slice_in_dim(block, 0, width, axis=dim), axis, backward)  5.17 us
    ppermute x4, waiting for transfers between devices, with_halo(): lax.ppermute(lax.slice_in_dim(block, block.shape[dim] - width, None, axis...  5.02 us
    dot_general x18, matrix products, conv_valid(): jnp.einsum('oc,hcw->how', kernel[3 * row_shift + col_shift], window, pref...  4.88 us
    unnamed x16, local copies, waits for them, and re-layouts  3.32 us
  transfers between devices with their start and end apart: 8, of which 5 were waited for; matrix products, arithmetic and copies ran while one was open for 2% of the time, Pallas kernels for 0%

profile of v1, /device:TPU:0, one launch (start us, length us, event | category | flops | bytes accessed | tf_op | source)
XLA Modules:
  0.0 121.4 jit_solution(4627882583251327285)
XLA Ops:
  0.0 0.8 fusion.97
  1.1 0.7 fusion.107
  1.8 0.7 multiply_add_fusion
  2.5 0.2 select_reduce_fusion
  2.7 0.7 fusion.102
  3.4 0.2 select_reduce_fusion.1
  3.6 0.7 add_add_fusion
  4.3 2.3 %copy-done = bf16[128,4,35,128]{3,1,2,0:T(4,128)(2,1)S(1)} copy-done((bf16[128,4,35,128]{3,1,2,0:T(4,128)(2,1)S(1)}, bf16[128,4,35,128]{3,1,2,0:T(4,128)(2,1)}, u32[]{:S(2)}) %copy-start) | copy-done | bytes 4587544
  6.6 0.9 copy-done.1
  7.5 52.9 %reduce_fragments.1 = (bf16[8,35,4,128]{3,2,1,0:T(4,128)(2,1)S(1)}, bf16[8,4,128]{2,1,0:T(4,128)(2,1)S(1)}) custom-call(s32[576]{0:T(1024)S(1)} %pad_add_fusion.tab, bf16[128,35,4,128]{3,2,1,0:T(4,128)(2,1)S(1)} %bitcast.101, bf16[128,4,128]{2,1,0:T(4,128)(2,1)S(1)} %copy-done.1), custom_call_target="tpu_custom_call" | custom-call | tf_op jit(solution)/shard_map/reduce_fragments/pallas_call | solution.py:404
  60.4 0.2 copy.30
  60.6 0.4 maximum_bitcast_fusion
  61.0 0.2 reshape.46
  61.3 1.3 %collective-permute-start = (bf16[1,36,256]{2,1,0:T(8,128)(2,1)S(1)}, bf16[1,36,256]{2,1,0:T(8,128)(2,1)S(1)}, u32[]{:S(2)}, u32[]{:S(2)}) collective-permute-start(bf16[1,36,256]{2,1,0:T(8,128)(2,1)S(1)} %get-tuple-element.12), channel_id=1, source_target_pairs={{0,16},{16,32},{32,48},{48,64},{64,80},{80,96},{96,112},{1,17},{17... | collective-permute-start | bytes 55304 | tf_op jit(solution)/shard_map/ppermute | solution.py:457
  62.6 1.3 %collective-permute-start.1 = (bf16[1,36,256]{2,1,0:T(8,128)(2,1)S(1)}, bf16[1,36,256]{2,1,0:T(8,128)(2,1)S(1)}, u32[]{:S(2)}, u32[]{:S(2)}) collective-permute-start(bf16[1,36,256]{2,1,0:T(8,128)(2,1)S(1)} %get-tuple-element.11), channel_id=1, source_target_pairs={{16,0},{32,16},{48,32},{64,48},{80,64},{96,80},{112,96},{17,1},{33... | collective-permute-start | bytes 55304 | tf_op jit(solution)/shard_map/ppermute | solution.py:460
  63.9 0.2 fusion.68
  64.4 1.3 %collective-permute-done.1 = bf16[1,36,256]{2,1,0:T(8,128)(2,1)S(1)} collective-permute-done((bf16[1,36,256]{2,1,0:T(8,128)(2,1)S(1)}, bf16[1,36,256]{2,1,0:T(8,128)(2,1)S(1)}, u32[]{:S(2)}, u32[]{:S(2)}) %collective-permute-start.1) | collective-permute-done | bytes 18464 | tf_op jit(solution)/shard_map/ppermute | solution.py:460
  65.8 1.3 %collective-permute-start.3 = (bf16[18,36,1]{2,1,0:T(8,128)(2,1)S(1)}, bf16[18,36,1]{2,1,0:T(8,128)(2,1)S(1)}, u32[]{:S(2)}, u32[]{:S(2)}) collective-permute-start(bf16[18,36,1]{2,1,0:T(8,128)(2,1)S(1)} %get-tuple-element.10), channel_id=1, source_target_pairs={{1,0},{2,1},{3,2},{4,3},{5,4},{6,5},{7,6},{8,7},{9,8},{10,9},{11,1... | collective-permute-start | bytes 3896 | tf_op jit(solution)/shard_map/ppermute | solution.py:460
  67.1 4.6 %collective-permute-start.2 = (bf16[18,36,1]{2,1,0:T(8,128)(2,1)S(1)}, bf16[18,36,1]{2,1,0:T(8,128)(2,1)S(1)}, u32[]{:S(2)}, u32[]{:S(2)}) collective-permute-start(bf16[18,36,1]{2,1,0:T(8,128)(2,1)S(1)} %get-tuple-element.9), channel_id=1, source_target_pairs={{0,1},{1,2},{2,3},{3,4},{4,5},{5,6},{6,7},{7,8},{8,9},{9,10},{10,1... | collective-permute-start | bytes 3896 | tf_op jit(solution)/shard_map/ppermute | solution.py:457
  71.7 0.2 fusion.18
  71.9 0.2 fusion.22
  72.1 4.1 %collective-permute-done.2 = bf16[18,36,1]{2,1,0:T(8,128)(2,1)S(1)} collective-permute-done((bf16[18,36,1]{2,1,0:T(8,128)(2,1)S(1)}, bf16[18,36,1]{2,1,0:T(8,128)(2,1)S(1)}, u32[]{:S(2)}, u32[]{:S(2)}) %collective-permute-start.2) | collective-permute-done | bytes 1328 | tf_op jit(solution)/shard_map/ppermute | solution.py:457
  76.2 0.3 fusion.32
  76.5 0.3 fusion.38
  76.8 0.3 fusion.29
  77.2 0.3 fusion.36
  77.5 0.4 fusion.7
  77.9 0.4 multiply_convert_fusion
  78.4 2.5 %collective-permute-start.4 = (bf16[1,32,256]{2,1,0:T(8,128)(2,1)S(1)}, bf16[1,32,256]{2,1,0:T(8,128)(2,1)S(1)}, u32[]{:S(2)}, u32[]{:S(2)}) collective-permute-start(bf16[1,32,256]{2,1,0:T(8,128)(2,1)S(1)} %get-tuple-element.17), channel_id=1, source_target_pairs={{0,16},{16,32},{32,48},{48,64},{64,80},{80,96},{96,112},{1,17},{17... | collective-permute-start | bytes 49160 | tf_op jit(solution)/shard_map/ppermute | solution.py:457
  80.9 1.3 %collective-permute-start.5 = (bf16[1,32,256]{2,1,0:T(8,128)(2,1)S(1)}, bf16[1,32,256]{2,1,0:T(8,128)(2,1)S(1)}, u32[]{:S(2)}, u32[]{:S(2)}) collective-permute-start(bf16[1,32,256]{2,1,0:T(8,128)(2,1)S(1)} %get-tuple-element.18), channel_id=1, source_target_pairs={{16,0},{32,16},{48,32},{64,48},{80,64},{96,80},{112,96},{17,1},{33... | collective-permute-start | bytes 49160 | tf_op jit(solution)/shard_map/ppermute | solution.py:460
  82.2 0.2 fusion.58
  82.4 1.6 %collective-permute-done.5 = bf16[1,32,256]{2,1,0:T(8,128)(2,1)S(1)} collective-permute-done((bf16[1,32,256]{2,1,0:T(8,128)(2,1)S(1)}, bf16[1,32,256]{2,1,0:T(8,128)(2,1)S(1)}, u32[]{:S(2)}, u32[]{:S(2)}) %collective-permute-start.5) | collective-permute-done | bytes 16416 | tf_op jit(solution)/shard_map/ppermute | solution.py:460
  84.2 4.4 %collective-permute-start.6 = (bf16[18,32,1]{2,1,0:T(8,128)(2,1)S(1)}, bf16[18,32,1]{2,1,0:T(8,128)(2,1)S(1)}, u32[]{:S(2)}, u32[]{:S(2)}) collective-permute-start(bf16[18,32,1]{2,1,0:T(8,128)(2,1)S(1)} %get-tuple-element.15), channel_id=1, source_target_pairs={{0,1},{1,2},{2,3},{3,4},{4,5},{5,6},{6,7},{7,8},{8,9},{9,10},{10,1... | collective-permute-start | bytes 3464 | tf_op jit(solution)/shard_map/ppermute | solution.py:457
  88.5 1.3 %collective-permute-start.7 = (bf16[18,32,1]{2,1,0:T(8,128)(2,1)S(1)}, bf16[18,32,1]{2,1,0:T(8,128)(2,1)S(1)}, u32[]{:S(2)}, u32[]{:S(2)}) collective-permute-start(bf16[18,32,1]{2,1,0:T(8,128)(2,1)S(1)} %get-tuple-element.16), channel_id=1, source_target_pairs={{1,0},{2,1},{3,2},{4,3},{5,4},{6,5},{7,6},{8,7},{9,8},{10,9},{11,1... | collective-permute-start | bytes 3464 | tf_op jit(solution)/shard_map/ppermute | solution.py:460
  89.8 0.2 fusion.51
  90.0 0.2 fusion.42
  90.2 0.9 collective-permute-done.6
  91.2 4.9 %collective-permute-done.7 = bf16[18,32,1]{2,1,0:T(8,128)(2,1)S(1)} collective-permute-done((bf16[18,32,1]{2,1,0:T(8,128)(2,1)S(1)}, bf16[18,32,1]{2,1,0:T(8,128)(2,1)S(1)}, u32[]{:S(2)}, u32[]{:S(2)}) %collective-permute-start.7) | collective-permute-done | bytes 1184 | tf_op jit(solution)/shard_map/ppermute | solution.py:460
  96.0 0.2 maximum_maximum_fusion
  96.3 0.3 fusion.49
  96.6 0.3 fusion.40
  96.8 0.2 fusion.47
  97.1 0.2 fusion.44
  97.3 0.2 fusion.10
  97.5 0.3 fusion.17
  97.9 0.6 gather_fusion
  98.4 22.0 %all_to_all.15 = bf16[16,32,256]{2,1,0:T(8,128)(2,1)S(1)} all-to-all(bf16[16,32,256]{2,1,0:T(8,128)(2,1)S(1)} %gather_fusion), channel_id=1, replica_groups=mesh['gx'=8,'gy'=16] {'gy'}, dimensions={0} | all-to-all | bytes 524288 | tf_op jit(solution)/shard_map/all_to_all | solution.py:518
  120.6 0.8 broadcast_in_dim.56
  (37 shorter events, 1.0 us)
Async XLA Ops:
  0.0 63.9 %copy-start.3 = (bf16[9,32,36]{2,1,0:T(8,128)(2,1)S(1)}, bf16[9,32,36]{2,1,0:T(8,128)(2,1)}, u32[]{:S(2)}) copy-start(bf16[9,32,36]{2,1,0:T(8,128)(2,1)} %param.22) | copy-start | bytes 62212
  0.0 64.2 %copy-start.5 = (s32[16]{0:T(128)S(1)}, s32[16]{0:T(128)}, u32[]{:S(2)}) copy-start(s32[16]{0:T(128)} %param.21) | copy-start | bytes 196
  4.3 2.3 %copy-start = (bf16[128,4,35,128]{3,1,2,0:T(4,128)(2,1)S(1)}, bf16[128,4,35,128]{3,1,2,0:T(4,128)(2,1)}, u32[]{:S(2)}) copy-start(bf16[128,4,35,128]{3,1,2,0:T(4,128)(2,1)} %param.17) | copy-start | bytes 13762564
  6.6 0.9 copy-start.1
  61.3 3.0 %collective-permute-start = (bf16[1,36,256]{2,1,0:T(8,128)(2,1)S(1)}, bf16[1,36,256]{2,1,0:T(8,128)(2,1)S(1)}, u32[]{:S(2)}, u32[]{:S(2)}) collective-permute-start(bf16[1,36,256]{2,1,0:T(8,128)(2,1)S(1)} %get-tuple-element.12), channel_id=1, source_target_pairs={{0,16},{16,32},{32,48},{48,64},{64,80},{80,96},{96,112},{1,17},{17... | collective-permute-start | bytes 55304 | tf_op jit(solution)/shard_map/ppermute | solution.py:457
  62.6 3.1 %collective-permute-start.1 = (bf16[1,36,256]{2,1,0:T(8,128)(2,1)S(1)}, bf16[1,36,256]{2,1,0:T(8,128)(2,1)S(1)}, u32[]{:S(2)}, u32[]{:S(2)}) collective-permute-start(bf16[1,36,256]{2,1,0:T(8,128)(2,1)S(1)} %get-tuple-element.11), channel_id=1, source_target_pairs={{16,0},{32,16},{48,32},{64,48},{80,64},{96,80},{112,96},{17,1},{33... | collective-permute-start | bytes 55304 | tf_op jit(solution)/shard_map/ppermute | solution.py:460
  65.8 11.0 %collective-permute-start.3 = (bf16[18,36,1]{2,1,0:T(8,128)(2,1)S(1)}, bf16[18,36,1]{2,1,0:T(8,128)(2,1)S(1)}, u32[]{:S(2)}, u32[]{:S(2)}) collective-permute-start(bf16[18,36,1]{2,1,0:T(8,128)(2,1)S(1)} %get-tuple-element.10), channel_id=1, source_target_pairs={{1,0},{2,1},{3,2},{4,3},{5,4},{6,5},{7,6},{8,7},{9,8},{10,9},{11,1... | collective-permute-start | bytes 3896 | tf_op jit(solution)/shard_map/ppermute | solution.py:460
  67.1 10.8 %copy-start.6 = (f32[32]{0:T(128)S(1)}, f32[32]{0:T(128)}, u32[]{:S(2)}) copy-start(f32[32]{0:T(128)} %param.23) | copy-start | bytes 388
  67.1 9.1 %collective-permute-start.2 = (bf16[18,36,1]{2,1,0:T(8,128)(2,1)S(1)}, bf16[18,36,1]{2,1,0:T(8,128)(2,1)S(1)}, u32[]{:S(2)}, u32[]{:S(2)}) collective-permute-start(bf16[18,36,1]{2,1,0:T(8,128)(2,1)S(1)} %get-tuple-element.9), channel_id=1, source_target_pairs={{0,1},{1,2},{2,3},{3,4},{4,5},{5,6},{6,7},{7,8},{8,9},{9,10},{10,1... | collective-permute-start | bytes 3896 | tf_op jit(solution)/shard_map/ppermute | solution.py:457
  76.8 5.4 %copy-start.2 = (bf16[9,32,32]{2,1,0:T(8,128)(2,1)S(1)}, bf16[9,32,32]{2,1,0:T(8,128)(2,1)}, u32[]{:S(2)}) copy-start(bf16[9,32,32]{2,1,0:T(8,128)(2,1)} %param.24) | copy-start | bytes 55300
  78.4 4.1 %collective-permute-start.4 = (bf16[1,32,256]{2,1,0:T(8,128)(2,1)S(1)}, bf16[1,32,256]{2,1,0:T(8,128)(2,1)S(1)}, u32[]{:S(2)}, u32[]{:S(2)}) collective-permute-start(bf16[1,32,256]{2,1,0:T(8,128)(2,1)S(1)} %get-tuple-element.17), channel_id=1, source_target_pairs={{0,16},{16,32},{32,48},{48,64},{64,80},{80,96},{96,112},{1,17},{17... | collective-permute-start | bytes 49160 | tf_op jit(solution)/shard_map/ppermute | solution.py:457
  80.9 3.1 %collective-permute-start.5 = (bf16[1,32,256]{2,1,0:T(8,128)(2,1)S(1)}, bf16[1,32,256]{2,1,0:T(8,128)(2,1)S(1)}, u32[]{:S(2)}, u32[]{:S(2)}) collective-permute-start(bf16[1,32,256]{2,1,0:T(8,128)(2,1)S(1)} %get-tuple-element.18), channel_id=1, source_target_pairs={{16,0},{32,16},{48,32},{64,48},{80,64},{96,80},{112,96},{17,1},{33... | collective-permute-start | bytes 49160 | tf_op jit(solution)/shard_map/ppermute | solution.py:460
  84.1 13.4 %copy-start.4 = (f32[32]{0:T(128)S(1)}, f32[32]{0:T(128)}, u32[]{:S(2)}) copy-start(f32[32]{0:T(128)} %param.25) | copy-start | bytes 388
  84.2 7.0 %collective-permute-start.6 = (bf16[18,32,1]{2,1,0:T(8,128)(2,1)S(1)}, bf16[18,32,1]{2,1,0:T(8,128)(2,1)S(1)}, u32[]{:S(2)}, u32[]{:S(2)}) collective-permute-start(bf16[18,32,1]{2,1,0:T(8,128)(2,1)S(1)} %get-tuple-element.15), channel_id=1, source_target_pairs={{0,1},{1,2},{2,3},{3,4},{4,5},{5,6},{6,7},{7,8},{8,9},{9,10},{10,1... | collective-permute-start | bytes 3464 | tf_op jit(solution)/shard_map/ppermute | solution.py:457
  88.5 7.5 %collective-permute-start.7 = (bf16[18,32,1]{2,1,0:T(8,128)(2,1)S(1)}, bf16[18,32,1]{2,1,0:T(8,128)(2,1)S(1)}, u32[]{:S(2)}, u32[]{:S(2)}) collective-permute-start(bf16[18,32,1]{2,1,0:T(8,128)(2,1)S(1)} %get-tuple-element.16), channel_id=1, source_target_pairs={{1,0},{2,1},{3,2},{4,3},{5,4},{6,5},{7,6},{8,7},{9,8},{10,9},{11,1... | collective-permute-start | bytes 3464 | tf_op jit(solution)/shard_map/ppermute | solution.py:460

commit v2 on v1

--- a/solution.py
+++ b/solution.py
@@ -42,7 +42,7 @@
     return flip4(c // SIDE, mask // SIDE) * SIDE + flip4(c % SIDE, mask % SIDE)
 
 
-def tables(footprints, depth_order, gx, gy):
+def tables(footprints, depth_order, panel_map, gx, gy):
     own = lax.dynamic_slice_in_dim(footprints, gx * NY + gy, 1, 0)[0]
     local = own % TILES
     slot = (own // TILES) % NY * TILES + local
@@ -87,7 +87,9 @@
     steps = jnp.tile(jnp.arange(DEPTH, dtype=jnp.int32), TILES)
     hit = (brick + 128 * which)[:, None] == listed[None, :]
     depth = jnp.sum(jnp.where(hit, steps[None, :] - (DEPTH + 1), 0), axis=1) + DEPTH + 1
-    return jnp.concatenate([pos, source.reshape(-1), which * TSTEP + depth])
+    panels = jnp.arange(NY, dtype=jnp.int32)
+    inverse = jnp.sum(jnp.where(panel_map[:, None] == panels[None, :], panels[:, None], 0), axis=0)
+    return jnp.concatenate([pos, source.reshape(-1), which * TSTEP + depth, inverse])
 
 
 POS_A = 0
@@ -95,12 +97,18 @@
 POS_S = 192
 SRC = 256
 RET = 384
-
-
-def reduce_kernel(
-    tab, pay_h, opa_h, comp, cov,
+INV = 576
+OUT = 32
+WIDE = 3 * COLS
+DEEP1 = (CH + 1) * ROWS
+DEEP2 = OUT * ROWS
+
+
+def frame_kernel(
+    tab, pay_h, opa_h, w1, b1, w2, b2, shown,
     pay, opa, asend, abuf, tb, tsend, trecv, s1, r1, s2, acc, r2, s3, r3, s4, r4, ys, yr,
-    lsem, a_s, a_r, t_s, t_r, m_s, m_r, y_s, y_r,
+    cov, stage, v1, pack, side, corner, band1, band2, h_acc, v2, v2_top, v2_low, o_acc, shaded, strips, got,
+    lsem, a_s, a_r, t_s, t_r, m_s, m_r, y_s, y_r, h_s, h_r, d_s, d_r,
 ):
     gx = lax.axis_index("gx")
     me = lax.axis_index("gy")
@@ -188,6 +196,8 @@
     for q in range(4):
         pack_raw(q, 0, 4)
 
+    spread_weights(w1, w2, band1, band2)
+
     def alpha_wait(n, _):
         col = (me + n) % NY
         for back in range(2):
@@ -219,7 +229,7 @@
         0, DEPTH, through, tuple(jnp.ones((ROWS, COLS), jnp.float32) for _ in range(TILES))
     )
     for t in range(TILES):
-        cov[t] = (1.0 - last[t]).astype(jnp.bfloat16)
+        cov[t] = 1.0 - last[t]
 
     def fill(i, _):
         tsend[i] = tb[tab[RET + i]]
@@ -364,6 +374,40 @@
         )
 
     cross = [cross_copy(q) for q in range(4)]
+    right = (me + 1) % NY
+    left = (me + NY - 1) % NY
+
+    def place(jy, j, v):
+        lanes = pl.ds(j * COLS, COLS)
+        for c in range(CH):
+            stage[jy, j, pl.ds(c * ROWS, ROWS), :] = v[c]
+        stage[jy, j, pl.ds(CH * ROWS, ROWS), :] = cov[jy * TXD + j]
+        v1[jy + 1, :, lanes] = stage[jy, j].astype(jnp.bfloat16)
+
+    def edge_copy(src, dst, n, row, col):
+        return pltpu.make_async_remote_copy(
+            src_ref=src,
+            dst_ref=dst,
+            send_sem=h_s.at[n],
+            recv_sem=h_r.at[n],
+            device_id=(row, col),
+            device_id_type=MESH,
+        )
+
+    mine = pl.ds(0, TXD * COLS)
+    low = pl.ds(0, COLS)
+    high = pl.ds(COLS, COLS)
+    edges = (
+        edge_copy(v1.at[4, :, mine], v1.at[0, :, mine], 0, up, me),
+        edge_copy(v1.at[4, :, high], corner.at[0], 1, up, right),
+        edge_copy(v1.at[4, :, low], corner.at[1], 2, up, left),
+        edge_copy(v1.at[1, :, mine], v1.at[5, :, mine], 3, down, me),
+        edge_copy(v1.at[1, :, high], corner.at[2], 4, down, right),
+        edge_copy(v1.at[1, :, low], corner.at[3], 5, down, left),
+        edge_copy(pack.at[0], side.at[0], 6, gx, right),
+        edge_copy(pack.at[1], side.at[1], 7, gx, left),
+    )
+
     for q in range(4):
         g, j = q // 2, q % 2
         four[q].wait_recv()
@@ -371,16 +415,172 @@
         ys[q, 1] = third.astype(jnp.bfloat16)
         if g == 0:
             ys[q, 0] = mid.astype(jnp.bfloat16)
-        else:
-            comp[3 * TXD + j] = mid.astype(jnp.bfloat16)
         cross[q].start()
         acc[q, 0, 0] = first
+        if g:
+            place(3, j, mid)
+    for n in range(3):
+        edges[n].start()
     for q in range(4):
         g, j = q // 2, q % 2
         cross[q].wait_recv()
-        comp[(1 + g) * TXD + j] = (acc[q, 0, 0] + yr[q, 1].astype(jnp.float32)).astype(jnp.bfloat16)
         if g == 0:
-            comp[j] = yr[q, 0]
+            place(0, j, yr[q, 0].astype(jnp.float32))
+        place(1 + g, j, acc[q, 0, 0] + yr[q, 1].astype(jnp.float32))
+        if q == 1:
+            for n in range(3, 6):
+                edges[n].start()
+
+    lane = lax.broadcasted_iota(jnp.int32, (DEEP1, COLS), 1)
+    to_right = stage[0, 1]
+    to_left = stage[0, 0]
+    for jy in range(1, TYD):
+        spot = (lane // 2) == (COLS // 2 - 1 - jy)
+        to_right = jnp.where(spot, pltpu.roll(stage[jy, 1], COLS - 2 * jy, 1), to_right)
+        spot = (lane // 2) == jy
+        to_left = jnp.where(spot, pltpu.roll(stage[jy, 0], 2 * jy, 1), to_left)
+    pack[0] = to_right.astype(jnp.bfloat16)
+    pack[1] = to_left.astype(jnp.bfloat16)
+    edges[6].start()
+    edges[7].start()
+    for copy in edges:
+        copy.wait_recv()
+
+    on_right = jnp.logical_and(lane < COLS // 2, me < NY - 1)
+    on_left = jnp.logical_and(lane >= COLS // 2, me > 0)
+    last_tile = pl.ds(2 * COLS, COLS)
+    zero = jnp.zeros((DEEP1, COLS), jnp.float32)
+    from_left = side[0].astype(jnp.float32)
+    from_right = side[1].astype(jnp.float32)
+    for jy in range(TYD):
+        r_part = pltpu.roll(from_right, COLS - 2 * jy, 1) if jy else from_right
+        l_part = pltpu.roll(from_left, 2 * jy, 1) if jy else from_left
+        rim = jnp.where(on_right, r_part, jnp.where(on_left, l_part, zero))
+        v1[jy + 1, :, last_tile] = rim.astype(jnp.bfloat16)
+    wide_zero = jnp.zeros((DEEP1, TXD * COLS), jnp.bfloat16)
+    for blk, base, inside in ((0, 0, gx > 0), (5, 2, gx < NX - 1)):
+        l_part = corner[base].astype(jnp.float32)
+        r_part = corner[base + 1].astype(jnp.float32)
+        rim = jnp.where(on_right, r_part, jnp.where(on_left, l_part, zero))
+        rim = jnp.where(inside, rim, zero)
+        v1[blk, :, last_tile] = rim.astype(jnp.bfloat16)
+
+        @pl.when(jnp.logical_not(inside))
+        def _(blk=blk):
+            v1[blk, :, mine] = wide_zero
+
+    def product(band, rows, field):
+        total = None
+        for dx in range(3):
+            z = jnp.dot(band(dx, rows), field, preferred_element_type=jnp.float32)
+            if dx != 1:
+                z = pltpu.roll(z, (1 - dx) % WIDE, 1)
+            total = z if total is None else total + z
+        return total
+
+    def band_one(dx, rows):
+        return band1[dx, rows, :]
+
+    def band_two(dx, rows):
+        return band2[dx, rows, :]
+
+    def column(ref):
+        eye = lax.broadcasted_iota(jnp.int32, (OUT, OUT), 0) == lax.broadcasted_iota(jnp.int32, (OUT, OUT), 1)
+        return jnp.sum(jnp.where(eye, ref[...], 0.0), axis=1, keepdims=True)
+
+    every = pl.ds(0, 6 * OUT)
+    head = product(band_one, pl.ds(4 * OUT, 2 * OUT), v1[0])
+    h_acc[0] = head[:OUT]
+    h_acc[1] = head[OUT:]
+    for blk in range(TYD):
+        s = product(band_one, every, v1[blk + 1])
+        y = 4 * blk
+        for n in range(6):
+            piece = s[n * OUT : (n + 1) * OUT]
+            h_acc[y + n] = piece + h_acc[y + n] if n < 2 else piece
+    tail = product(band_one, pl.ds(0, 2 * OUT), v1[5])
+    bias_one = column(b1)
+    far = lax.broadcasted_iota(jnp.int32, (OUT, WIDE), 1)
+    cut = jnp.logical_or(
+        jnp.logical_and(far >= 2 * COLS + COLS // 2, me == 0),
+        jnp.logical_and(
+            jnp.logical_and(far >= 2 * COLS, far < 2 * COLS + COLS // 2), me == NY - 1
+        ),
+    )
+    for n in range(18):
+        raw_sum = h_acc[n]
+        if n >= 16:
+            raw_sum = raw_sum + tail[(n - 16) * OUT : (n - 15) * OUT]
+        pre = raw_sum + bias_one
+        h = pre * lax.logistic(pre)
+        h = jnp.where(cut, 0.0, h)
+        if n == 0:
+            v2_top[...] = jnp.where(gx > 0, h, 0.0).astype(jnp.bfloat16)
+        elif n == 17:
+            v2_low[...] = jnp.where(gx < NX - 1, h, 0.0).astype(jnp.bfloat16)
+        else:
+            v2[(n - 1) // 4, pl.ds((n - 1) % 4 * OUT, OUT), :] = h.astype(jnp.bfloat16)
+
+    o_acc[0] = product(lambda dx, rows: w2[dx], every, v2_top[...])[:, : TXD * COLS]
+    for blk in range(TYD):
+        s = product(band_two, every, v2[blk])[:, : TXD * COLS]
+        y = 4 * blk - 1
+        for n in range(6):
+            piece = s[n * OUT : (n + 1) * OUT]
+            if 0 <= y + n < 16:
+                o_acc[y + n] = piece + o_acc[y + n] if n < 2 else piece
+    tail = product(lambda dx, rows: w2[6 + dx], every, v2_low[...])[:, : TXD * COLS]
+    bias_two = column(b2)
+    for n in range(16):
+        rows = pl.ds(n % 4, OUT, stride=ROWS)
+        base = jnp.concatenate([stage[n // 4, j, rows, :] for j in range(TXD)], axis=1)
+        value = o_acc[n] + bias_two + base.astype(jnp.bfloat16).astype(jnp.float32)
+        if n == 15:
+            value = value + tail
+        shaded[n] = value.astype(jnp.bfloat16)
+
+    def strip_copy(g):
+        return pltpu.make_async_remote_copy(
+            src_ref=strips.at[g],
+            dst_ref=got.at[me],
+            send_sem=d_s.at[g],
+            recv_sem=d_r.at[me],
+            device_id=(gx, g),
+            device_id_type=MESH,
+        )
+
+    def strip_start(n, _):
+        g = (me + n) % NY
+        strips[g] = shaded[tab[INV + g]]
+        strip_copy(g).start()
+        return 0
+
+    lax.fori_loop(1, NY, strip_start, 0)
+    got[me] = shaded[tab[INV + me]]
+
+    def strip_wait(n, _):
+        col = (me + n) % NY
+        pltpu.make_async_remote_copy(
+            src_ref=strips.at[col],
+            dst_ref=got.at[col],
+            send_sem=d_s.at[col],
+            recv_sem=d_r.at[col],
+            device_id=(gx, col),
+            device_id_type=MESH,
+        ).wait_recv()
+        return 0
+
+    lax.fori_loop(1, NY, strip_wait, 0)
+    for col in range(NY):
+        shown[:, pl.ds(col * TXD * COLS, TXD * COLS)] = got[col]
+
+    def strip_sent(n, _):
+        strip_copy((me + n) % NY).wait_send()
+        return 0
+
+    lax.fori_loop(1, NY, strip_sent, 0)
+    for copy in edges:
+        copy.wait_send()
 
     def alpha_sent(n, _):
         alpha_copy((me + n) % NY, 0).wait_send()
@@ -396,24 +596,43 @@
             copy.wait_send()
 
 
-def reduce_fragments(tab, payload, opacity):
+def spread_weights(w1, w2, band1, band2):
+    for ref, band, ins, wide, step in ((w1, band1, CH + 1, DEEP1, 4), (w2, band2, OUT, DEEP2, 1)):
+        chan = lax.broadcasted_iota(jnp.int32, (ins, wide), 0)
+        spot = lax.broadcasted_iota(jnp.int32, (ins, wide), 1)
+        pick = []
+        for r in range(ROWS):
+            where = chan * ROWS + r if step == 4 else chan + OUT * r
+            pick.append(jnp.where(spot == where, 1.0, 0.0).astype(jnp.bfloat16))
+        for dx in range(3):
+            for n in range(6):
+                total = None
+                for dy in range(3):
+                    r = n - 1 + dy - 1
+                    if 0 <= r < ROWS:
+                        term = jnp.dot(
+                            ref[3 * dy + dx], pick[r], preferred_element_type=jnp.float32
+                        )
+                        total = term if total is None else total + term
+                band[dx, pl.ds(n * OUT, OUT), :] = total.astype(jnp.bfloat16)
+
+
+def frame(tab, payload, opacity, w1, b1, w2, b2):
     unit = (CH, ROWS, COLS)
     bf16, f32 = jnp.bfloat16, jnp.float32
     vmem = pltpu.VMEM
     dma = pltpu.SemaphoreType.DMA
     return pl.pallas_call(
-        reduce_kernel,
-        name="reduce_fragments",
-        out_shape=(
-            jax.ShapeDtypeStruct((TILES,) + unit, bf16),
-            jax.ShapeDtypeStruct((TILES, ROWS, COLS), bf16),
-        ),
+        frame_kernel,
+        name="frame",
+        out_shape=jax.ShapeDtypeStruct((OUT, NY * TXD * COLS), bf16),
         in_specs=[
             pl.BlockSpec(memory_space=pltpu.SMEM),
             pl.BlockSpec(memory_space=pl.ANY),
             pl.BlockSpec(memory_space=pl.ANY),
-        ],
-        out_specs=(pl.BlockSpec(memory_space=vmem), pl.BlockSpec(memory_space=vmem)),
+        ]
+        + [pl.BlockSpec(memory_space=vmem)] * 4,
+        out_specs=pl.BlockSpec(memory_space=vmem),
         scratch_shapes=[
             vmem((128,) + unit, bf16),
             vmem((128, ROWS, COLS), bf16),
@@ -433,6 +652,22 @@
             vmem((4, 1, 3) + unit, bf16),
             vmem((4, 2) + unit, bf16),
             vmem((4, 2) + unit, bf16),
+            vmem((TILES, ROWS, COLS), f32),
+            vmem((TYD, TXD, DEEP1, COLS), f32),
+            vmem((TYD + 2, DEEP1, WIDE), bf16),
+            vmem((2, DEEP1, COLS), bf16),
+            vmem((2, DEEP1, COLS), bf16),
+            vmem((4, DEEP1, COLS), bf16),
+            vmem((3, 6 * OUT, DEEP1), bf16),
+            vmem((3, 6 * OUT, DEEP2), bf16),
+            vmem((18, OUT, WIDE), f32),
+            vmem((TYD, DEEP2, WIDE), bf16),
+            vmem((OUT, WIDE), bf16),
+            vmem((OUT, WIDE), bf16),
+            vmem((16, OUT, TXD * COLS), f32),
+            vmem((16, OUT, TXD * COLS), bf16),
+            vmem((NY, OUT, TXD * COLS), bf16),
+            vmem((NY, OUT, TXD * COLS), bf16),
             dma((5,)),
             dma((32,)),
             dma((32,)),
@@ -442,81 +677,32 @@
             dma((4, 10)),
             dma((4,)),
             dma((4,)),
+            dma((8,)),
+            dma((8,)),
+            dma((NY,)),
+            dma((NY,)),
         ],
         compiler_params=pltpu.CompilerParams(
             collective_id=0, has_side_effects=True, vmem_limit_bytes=48 << 20
         ),
-    )(tab, payload, opacity)
-
-
-def with_halo(block, sides, width):
-    for axis, dim in sides:
-        count = lax.axis_size(axis)
-        forward = [(i, i + 1) for i in range(count - 1)]
-        backward = [(target, source) for source, target in forward]
-        low = lax.ppermute(
-            lax.slice_in_dim(block, block.shape[dim] - width, None, axis=dim), axis, forward
-        )
-        high = lax.ppermute(lax.slice_in_dim(block, 0, width, axis=dim), axis, backward)
-        block = jnp.concatenate([low, block, high], axis=dim)
-    return block
-
-
-def conv_valid(padded, kernel):
-    height = padded.shape[0] - 2
-    span_cols = padded.shape[2] - 2
-    total = jnp.zeros((height, kernel.shape[1], span_cols), jnp.float32)
-    for row_shift in range(3):
-        for col_shift in range(3):
-            window = padded[row_shift : row_shift + height, :, col_shift : col_shift + span_cols]
-            total = total + jnp.einsum(
-                "oc,hcw->how",
-                kernel[3 * row_shift + col_shift],
-                window,
-                preferred_element_type=jnp.float32,
-            )
-    return total
-
-
-def rimmed(field):
-    return with_halo(field, (("gx", 0), ("gy", 2)), 1)
-
-
-def composited(payload, opacity, depth_order, footprints):
-    gx = lax.axis_index("gx")
-    gy = lax.axis_index("gy")
-    tab = tables(footprints, depth_order, gx, gy)
-    color, cover = reduce_fragments(tab, payload.transpose(0, 2, 1, 3), opacity)
-    composite = jnp.concatenate([color, cover[:, None]], axis=1)
-    region = composite.reshape(TYD, TXD, CH + 1, ROWS, COLS).transpose(0, 3, 2, 1, 4)
-    return region.reshape(TYD * ROWS, CH + 1, TXD * COLS)
+    )(tab, payload, opacity, w1, b1, w2, b2)
 
 
 def shards(
     payload, opacity, depth_order, footprints, panel_map,
     conv1_weight, conv1_bias, conv2_weight, conv2_bias,
 ):
-    col_groups = lax.axis_size("gy")
-    region = composited(payload, opacity, depth_order, footprints)
-    band_rows = region.shape[0]
-    region_cols = region.shape[2]
-    bias_one = conv1_bias[None, :, None]
-    bias_two = conv2_bias[None, :, None]
-    hidden = jax.nn.silu(conv_valid(rimmed(region), conv1_weight) + bias_one).astype(jnp.bfloat16)
-    shaded = conv_valid(rimmed(hidden), conv2_weight)
-    feature_count = conv2_weight.shape[1]
-    shaded = (shaded + bias_two + region[:, :feature_count, :].astype(jnp.float32)).astype(
-        jnp.bfloat16
+    tab = tables(footprints, depth_order, panel_map, lax.axis_index("gx"), lax.axis_index("gy"))
+    shown = frame(
+        tab,
+        payload.transpose(0, 2, 1, 3),
+        opacity,
+        conv1_weight,
+        conv1_bias[None],
+        conv2_weight,
+        conv2_bias[None],
     )
-    strip_rows = band_rows // col_groups
-    panel_range = jnp.arange(col_groups, dtype=jnp.int32)
-    inverse = jnp.sum(
-        jnp.where(panel_map[:, None] == panel_range[None, :], panel_range[:, None], 0), axis=0
-    )
-    pieces = shaded.reshape(col_groups, strip_rows, feature_count, region_cols)[inverse]
-    pieces = pieces.reshape(band_rows, feature_count, region_cols)
-    shown = lax.all_to_all(pieces, "gy", split_axis=0, concat_axis=2, tiled=True)
-    return shown[None, None]
+    return shown[None, None, None]
 
 
 SPECS = (

time: 123 us -> 78.2 us (0.64); the launches traced: 121 us -> 77.9 us
  blocking collectives: 22 us -> 0 us
  starting transfers between devices: 17.9 us -> 0 us
  Pallas kernels: 52.9 us -> 65.8 us
  waiting for transfers between devices: 12.7 us -> 0 us
  matrix products: 4.88 us -> 0 us
  local copies, waits for them, and re-layouts: 5.88 us -> 7.23 us
    all_to_all x1 -> x0, blocking collectives: 22 us -> none  [shards(): lax.all_to_all(pieces, 'gy', split_axis=0, concat_axis=2, tiled=True)]
    ppermute x8 -> x0, starting transfers between devices: 17.9 us -> none  [the longest x4 12.7 us: with_halo(): lax.ppermute(lax.slice_in_dim(block, block.shape[dim] - width, None, axis...]
    pallas_call x1, Pallas kernels: 52.9 us -> 65.8 us  [frame(): pl.pallas_call(frame_kernel, name='frame', out_shape=jax.ShapeDtypeStruct...]
    ppermute x8 -> x0, waiting for transfers between devices: 12.7 us -> none  [the longest x4 7.72 us: with_halo(): lax.ppermute(lax.slice_in_dim(block, 0, width, axis=dim), axis, backward)]
    dot_general x18 -> x0, matrix products: 4.88 us -> none  [conv_valid(): jnp.einsum('oc,hcw->how', kernel[3 * row_shift + col_shift], window, pref...]
    unnamed x16 -> x13, local copies, waits for them, and re-layouts: 3.32 us -> 6.98 us
  transfers between devices with their start and end apart: 8 -> 0, of which waited for: 5 -> 0; matrix products, arithmetic and copies ran while one was open for 2% -> 0% of each run, Pallas kernels for 0% -> 0%
where the time goes in v2:
time: 78.2 us; the launch traced here: 77.9 us
  Pallas kernels  65.8 us (84%)
  local copies, waits for them, and re-layouts  7.23 us (9%)
  other arithmetic  4.79 us (6%)
    pallas_call x1, Pallas kernels, frame(): pl.pallas_call(frame_kernel, name='frame', out_shape=jax.ShapeDtypeStruct...  65.8 us
    unnamed x13, local copies, waits for them, and re-layouts  6.98 us

profile of v2, /device:TPU:0, one launch (start us, length us, event | category | flops | bytes accessed | tf_op | source)
XLA Modules:
  0.0 77.9 jit_solution(12054400951339356141)
XLA Ops:
  0.0 0.7 fusion.14
  0.7 0.7 multiply_add_fusion
  1.4 0.7 fusion.10
  2.1 0.7 select_reduce_fusion.2
  2.9 0.2 select_reduce_fusion
  3.1 0.1 sub.37
  3.2 0.8 %fusion.5 = (s32[8,16]{1,0:T(8,128)S(1)}, s32[8,16]{1,0:T(8,128)S(1)}) fusion(s32[8,16]{1,0:T(8,128)} %param.19, s32[8]{0:T(128)} %constant.125, s32[8]{0:T(128)} %constant.124, s32[]{:T(128)S(6)} %axis_index.25, s32[8]{0:T(128)S(1)} %iota_multiply_fusion), kind=kLoop, calls=%fused_computation.17 | loop fusion | flops 4992 | bytes 1636 | tf_op jit(solution)/shard_map/add | solution.py:68
  3.9 0.1 reshape.16
  4.0 0.1 eq.56
  4.1 0.2 select_reduce_fusion.1
  4.3 0.7 add_add_fusion
  5.0 0.1 pad_add_fusion.tab
  5.1 0.0 copy-start
  5.1 2.3 %copy-done = bf16[128,4,35,128]{3,1,2,0:T(4,128)(2,1)S(1)} copy-done((bf16[128,4,35,128]{3,1,2,0:T(4,128)(2,1)S(1)}, bf16[128,4,35,128]{3,1,2,0:T(4,128)(2,1)}, u32[]{:S(2)}) %copy-start) | copy-done | bytes 4587544
  7.4 0.0 copy-start.1
  7.4 0.9 %copy-done.1 = bf16[128,4,128]{2,1,0:T(4,128)(2,1)S(1)} copy-done((bf16[128,4,128]{2,1,0:T(4,128)(2,1)S(1)}, bf16[128,4,128]{2,1,0:T(4,128)(2,1)}, u32[]{:S(2)}) %copy-start.1) | copy-done | bytes 131096
  8.3 0.0 copy-start.2
  8.3 0.9 %copy-done.2 = bf16[9,32,36]{2,1,0:T(8,128)(2,1)S(1)} copy-done((bf16[9,32,36]{2,1,0:T(8,128)(2,1)S(1)}, bf16[9,32,36]{2,1,0:T(8,128)(2,1)}, u32[]{:S(2)}) %copy-start.2) | copy-done | bytes 20760
  9.1 0.0 copy-start.3
  9.2 0.9 %copy-done.3 = bf16[9,32,32]{2,1,0:T(8,128)(2,1)S(1)} copy-done((bf16[9,32,32]{2,1,0:T(8,128)(2,1)S(1)}, bf16[9,32,32]{2,1,0:T(8,128)(2,1)}, u32[]{:S(2)}) %copy-start.3) | copy-done | bytes 18456
  10.0 0.0 copy-start.4
  10.0 0.7 copy-done.4
  10.7 0.0 copy-start.5
  10.7 0.7 copy-done.5
  11.3 65.8 %frame.1 = bf16[32,4096]{1,0:T(8,128)(2,1)S(1)} custom-call(s32[592]{0:T(1024)S(1)} %pad_add_fusion.tab, bf16[128,35,4,128]{3,2,1,0:T(4,128)(2,1)S(1)} %bitcast.6, bf16[128,4,128]{2,1,0:T(4,128)(2,1)S(1)} %copy-done.1, bf16[9,32,36]{2,1,0:T(8,128)(2,1)S(1)} %copy-done.2, f32[1,32]{1,0:T(1,128)S(1)} %bitcast.8, bf16[9,32,32]{2,1,0:T(8,128)(2,1)S(1)} %copy-done.3, ...), custom_call_target="tpu_custom_call" | custom-call | tf_op jit(solution)/shard_map/frame/pallas_call | solution.py:625
  77.2 0.7 copy.19
  (4 shorter events, 0.0 us)
Async XLA Ops:
  5.1 2.3 %copy-start = (bf16[128,4,35,128]{3,1,2,0:T(4,128)(2,1)S(1)}, bf16[128,4,35,128]{3,1,2,0:T(4,128)(2,1)}, u32[]{:S(2)}) copy-start(bf16[128,4,35,128]{3,1,2,0:T(4,128)(2,1)} %param.17) | copy-start | bytes 13762564
  7.4 0.9 %copy-start.1 = (bf16[128,4,128]{2,1,0:T(4,128)(2,1)S(1)}, bf16[128,4,128]{2,1,0:T(4,128)(2,1)}, u32[]{:S(2)}) copy-start(bf16[128,4,128]{2,1,0:T(4,128)(2,1)} %opa_h.1) | copy-start | bytes 393220
  8.3 0.9 %copy-start.2 = (bf16[9,32,36]{2,1,0:T(8,128)(2,1)S(1)}, bf16[9,32,36]{2,1,0:T(8,128)(2,1)}, u32[]{:S(2)}) copy-start(bf16[9,32,36]{2,1,0:T(8,128)(2,1)} %w1.1) | copy-start | bytes 62212
  9.1 0.9 %copy-start.3 = (bf16[9,32,32]{2,1,0:T(8,128)(2,1)S(1)}, bf16[9,32,32]{2,1,0:T(8,128)(2,1)}, u32[]{:S(2)}) copy-start(bf16[9,32,32]{2,1,0:T(8,128)(2,1)} %w2.1) | copy-start | bytes 55300
  10.0 0.7 copy-start.4
  10.7 0.7 copy-start.5

commit v3 on v2

--- a/solution.py
+++ b/solution.py
@@ -42,70 +42,72 @@
     return flip4(c // SIDE, mask // SIDE) * SIDE + flip4(c % SIDE, mask % SIDE)
 
 
-def tables(footprints, depth_order, panel_map, gx, gy):
-    own = lax.dynamic_slice_in_dim(footprints, gx * NY + gy, 1, 0)[0]
-    local = own % TILES
-    slot = (own // TILES) % NY * TILES + local
+def patterns():
     base = np.zeros((2, 4, 8, 2), np.int32)
     rest = np.zeros((2, 4, 8, 2), np.int32)
-    for role in range(2):
-        for q in range(4):
-            for k in range(8):
+    mask = np.zeros((4, 8, 3, 2), np.int32)
+    which = np.zeros((4, 8, 3, 2), np.int32)
+    for q in range(4):
+        j, g = q % 2, q // 2
+        for k in range(8):
+            for s in range(2):
+                flip = kappa(q, k) ^ (MASKS[q][0] if s else 0)
                 for f in range(2):
-                    j, g = q % 2, q // 2
                     jy = (1 + g) if f else (3 if g else 0)
-                    base[role, q, k, f] = kappa(q, k) ^ (MASKS[q][0] if role else 0)
-                    rest[role, q, k, f] = jy * TXD + j
-    owner = jnp.bitwise_xor(jnp.asarray(base.reshape(-1)), gy)
-    target = jnp.concatenate(
-        [jnp.arange(128, dtype=jnp.int32), owner * TILES + jnp.asarray(rest.reshape(-1))]
-    )
-    order = jnp.arange(128, dtype=jnp.int32)
-    pos = jnp.sum(jnp.where(target[:, None] == slot[None, :], order[None, :], 0), axis=1)
-
-    tile = np.arange(TILES, dtype=np.int32)[:, None]
-    part = (gx - depth_order // NY) % NX
-    source = (part * NY + depth_order % NY) * 6 + (tile // TXD - 1 + part) * TXD + tile % TXD
-
-    mask = np.zeros((4, 8, 3, 2), np.int32)
-    back = np.zeros((4, 8, 3, 2), np.int32)
-    which = np.zeros((4, 8, 3, 2), np.int32)
-    for q in range(4):
-        for k in range(8):
-            for e in range(3):
-                for s in range(2):
-                    j, g = q % 2, q // 2
+                    base[s, q, k, f] = flip
+                    rest[s, q, k, f] = jy * TXD + j
+                for e in range(3):
                     jy = (1 + g) if e != 1 else (3 if g else 0)
-                    back[q, k, e, s] = (0, 1 - g, 1)[e]
-                    mask[q, k, e, s] = kappa(q, k) ^ (MASKS[q][0] if s else 0)
-                    which[q, k, e, s] = jy * TXD + j
-    brick = (gx - jnp.asarray(back.reshape(-1))) % NX * NY + jnp.bitwise_xor(
-        jnp.asarray(mask.reshape(-1)), gy
-    )
-    which = jnp.asarray(which.reshape(-1))
-    listed = (depth_order + 128 * tile).reshape(-1)
-    steps = jnp.tile(jnp.arange(DEPTH, dtype=jnp.int32), TILES)
-    hit = (brick + 128 * which)[:, None] == listed[None, :]
-    depth = jnp.sum(jnp.where(hit, steps[None, :] - (DEPTH + 1), 0), axis=1) + DEPTH + 1
-    panels = jnp.arange(NY, dtype=jnp.int32)
-    inverse = jnp.sum(jnp.where(panel_map[:, None] == panels[None, :], panels[:, None], 0), axis=0)
-    return jnp.concatenate([pos, source.reshape(-1), which * TSTEP + depth, inverse])
-
-
-POS_A = 0
-POS_K = 128
-POS_S = 192
-SRC = 256
-RET = 384
-INV = 576
+                    mask[q, k, e, s] = flip
+                    which[q, k, e, s] = jy * TXD + j + TILES * (0, 1 - g, 1)[e]
+    rows = np.zeros((8, 128), np.int32)
+    rows[0] = base.reshape(-1)
+    rows[1] = rest.reshape(-1)
+    rows[2:4].reshape(-1)[:192] = mask.reshape(-1)
+    rows[4:6].reshape(-1)[:192] = which.reshape(-1)
+    return rows
+
+
+def fill_tables(rows, foot, order, out, gx, gy):
+    i32 = jnp.int32
+    own = foot[pl.ds(gx * NY + gy, 1), :]
+    slot = ((own >> 3) & (NY - 1)) * TILES + (own & (TILES - 1))
+    across = lax.broadcasted_iota(i32, (128, 128), 1)
+    along = lax.broadcasted_iota(i32, (128, 128), 0)
+    slots = jnp.sum(jnp.where(across == along, slot, 0), axis=1, keepdims=True)
+    target = (rows[0:1] ^ gy) * TILES + rows[1:2]
+    out[0:1] = jnp.max(jnp.where(slots == across, along, 0), axis=0, keepdims=True)
+    out[1:2] = jnp.max(jnp.where(slots == target, along, 0), axis=0, keepdims=True)
+
+    listed = order[...]
+    tile = lax.broadcasted_iota(i32, (TILES, 128), 0)
+    for n in range(2):
+        which = rows[4 + n : 5 + n]
+        local = which & (TILES - 1)
+        brick = ((gx - (which >> 3)) & (NX - 1)) * NY + (rows[2 + n : 3 + n] ^ gy)
+        rank = jnp.zeros((TILES, 128), i32)
+        for d in range(DEPTH):
+            hit = jnp.logical_and(listed[:, d : d + 1] == brick, tile == local)
+            rank = jnp.minimum(rank, jnp.where(hit, d - (DEPTH + 1), 0))
+        rank = jnp.min(rank, axis=0, keepdims=True)
+        out[2 + n : 3 + n] = local * TSTEP + DEPTH + 1 + rank
+
+    tile = lax.broadcasted_iota(i32, (TILES, DEPTH), 0)
+    part = jnp.minimum((gx - (listed >> 4)) & (NX - 1), 1)
+    spot = ((tile >> 1) - 1 + part) * TXD + (tile & 1)
+    out[8:16, 0:DEPTH] = jnp.maximum((part * NY + (listed & (NY - 1))) * 6 + spot, 0)
+
+
 OUT = 32
+VMEM_BYTES = 62 << 20
 WIDE = 3 * COLS
 DEEP1 = (CH + 1) * ROWS
 DEEP2 = OUT * ROWS
 
 
 def frame_kernel(
-    tab, pay_h, opa_h, w1, b1, w2, b2, shown,
+    pay_h, opa_h, rows_h, foot_h, order_h, panel_h, w1_h, b1_h, w2_h, b2_h, shown,
+    rows, foot, order, tabv, tab, panel, inv, w1, b1, w2, b2, tsem,
     pay, opa, asend, abuf, tb, tsend, trecv, s1, r1, s2, acc, r2, s3, r3, s4, r4, ys, yr,
     cov, stage, v1, pack, side, corner, band1, band2, h_acc, v2, v2_top, v2_low, o_acc, shaded, strips, got,
     lsem, a_s, a_r, t_s, t_r, m_s, m_r, y_s, y_r, h_s, h_r, d_s, d_r,
@@ -114,11 +116,18 @@
     me = lax.axis_index("gy")
     up = (gx + 1) % NX
     down = (gx + NX - 1) % NX
-    loads = [pltpu.make_async_copy(opa_h, opa, lsem.at[4])]
+    early = [
+        pltpu.make_async_copy(src, dst, tsem.at[n])
+        for n, (src, dst) in enumerate(
+            ((rows_h, rows), (foot_h, foot), (order_h, order), (opa_h, opa), (panel_h, panel),
+             (w1_h, w1), (b1_h, b1), (w2_h, w2), (b2_h, b2))
+        )
+    ]
+    loads = []
     for i in range(4):
         part = pl.ds(32 * i, 32)
         loads.append(pltpu.make_async_copy(pay_h.at[part], pay.at[part], lsem.at[i]))
-    for load in loads:
+    for load in early[:4] + loads + early[4:]:
         load.start()
 
     barrier = pltpu.get_barrier_semaphore()
@@ -135,15 +144,34 @@
     lax.fori_loop(1, NY, greet_row, 0)
     lax.fori_loop(0, NY, greet_next, 0)
 
-    loads[0].wait()
+    for load in early[:3]:
+        load.wait()
+    fill_tables(rows, foot, order, tabv, gx, me)
+    to_smem = pltpu.make_async_copy(tabv, tab, tsem.at[9])
+    early[3].wait()
+    to_smem.start()
+    to_smem.wait()
 
     def pack_alpha(i, _):
-        asend[i] = opa[tab[POS_A + i]]
+        asend[i] = opa[tab[0, i]]
         return 0
 
     lax.fori_loop(0, 128, pack_alpha, 0, unroll=8)
     for e in range(6):
         abuf[me * 6 + e] = asend[me * TILES + 2 + e]
+    for load in loads:
+        load.wait()
+
+    def pack_raw(q, lo, hi):
+        def body(k, _):
+            for f in range(2):
+                s1[q, k, f] = pay[tab[1, 64 + (q * 8 + k) * 2 + f]]
+            return 0
+
+        lax.fori_loop(lo, hi, body, 0)
+
+    for q in range(4):
+        pack_raw(q, 2, 8)
     pl.semaphore_wait(barrier, 47)
 
     def alpha_copy(i, back):
@@ -163,17 +191,6 @@
 
     lax.fori_loop(1, NY, alpha_start, 0)
     alpha_copy(me, 1).start()
-
-    for load in loads[1:]:
-        load.wait()
-
-    def pack_raw(q, lo, hi):
-        def body(k, _):
-            for f in range(2):
-                s1[q, k, f] = pay[tab[POS_S + (q * 8 + k) * 2 + f]]
-            return 0
-
-        lax.fori_loop(lo, hi, body, 0)
 
     groups = ((4, 8), (2, 4), (1, 2), (0, 1))
 
@@ -190,11 +207,22 @@
         )
 
     raw = [[raw_copy(q, n) for n in range(4)] for q in range(4)]
-    for q in range(4):
-        pack_raw(q, 4, 8)
-        raw[q][0].start()
-    for q in range(4):
-        pack_raw(q, 0, 4)
+    for n in range(2):
+        for q in range(4):
+            raw[q][n].start()
+    for q in range(4):
+        pack_raw(q, 0, 2)
+    for load in early[4:]:
+        load.wait()
+
+    def invert(g, _):
+        at = 0
+        for strip in range(NY):
+            at = jnp.where(panel[strip] == g, strip, at)
+        inv[g] = at
+        return 0
+
+    lax.fori_loop(0, NY, invert, 0)
 
     spread_weights(w1, w2, band1, band2)
 
@@ -221,7 +249,7 @@
         out = []
         for t in range(TILES):
             tb[t * TSTEP + d] = passed[t]
-            alpha = abuf[tab[SRC + t * DEPTH + d]].astype(jnp.float32)
+            alpha = abuf[tab[8 + t, d]].astype(jnp.float32)
             out.append(passed[t] * (1.0 - alpha))
         return tuple(out)
 
@@ -232,7 +260,7 @@
         cov[t] = 1.0 - last[t]
 
     def fill(i, _):
-        tsend[i] = tb[tab[RET + i]]
+        tsend[i] = tb[tab[2 + i // 128, i % 128]]
         return 0
 
     lax.fori_loop(0, 192, fill, 0, unroll=8)
@@ -264,17 +292,17 @@
                 else:
                     weights[q, k, back] = weight_copy(q, k, back)
                     weights[q, k, back].start()
-    for q in range(4):
-        for n in range(1, 4):
+    for n in range(2, 4):
+        for q in range(4):
             raw[q][n].start()
 
     def weighed(q, k):
         own = (q * 8 + k) * 2
         lead = (q * 8 + k) * 6
-        own_f = pay[tab[POS_K + own]].astype(jnp.float32)
+        own_f = pay[tab[1, own]].astype(jnp.float32)
         got_f = r1[q, k, 0].astype(jnp.float32)
         mid = trecv[lead + 2][None] * own_f + trecv[lead + 3][None] * got_f
-        own_a = pay[tab[POS_K + own + 1]].astype(jnp.float32)
+        own_a = pay[tab[1, own + 1]].astype(jnp.float32)
         got_a = r1[q, k, 1].astype(jnp.float32)
         first = trecv[lead][None] * own_a + trecv[lead + 1][None] * got_a
         third = trecv[lead + 4][None] * own_a + trecv[lead + 5][None] * got_a
@@ -551,12 +579,12 @@
 
     def strip_start(n, _):
         g = (me + n) % NY
-        strips[g] = shaded[tab[INV + g]]
+        strips[g] = shaded[inv[g]]
         strip_copy(g).start()
         return 0
 
     lax.fori_loop(1, NY, strip_start, 0)
-    got[me] = shaded[tab[INV + me]]
+    got[me] = shaded[inv[me]]
 
     def strip_wait(n, _):
         col = (me + n) % NY
@@ -617,7 +645,7 @@
                 band[dx, pl.ds(n * OUT, OUT), :] = total.astype(jnp.bfloat16)
 
 
-def frame(tab, payload, opacity, w1, b1, w2, b2):
+def frame(*operands):
     unit = (CH, ROWS, COLS)
     bf16, f32 = jnp.bfloat16, jnp.float32
     vmem = pltpu.VMEM
@@ -626,14 +654,21 @@
         frame_kernel,
         name="frame",
         out_shape=jax.ShapeDtypeStruct((OUT, NY * TXD * COLS), bf16),
-        in_specs=[
-            pl.BlockSpec(memory_space=pltpu.SMEM),
-            pl.BlockSpec(memory_space=pl.ANY),
-            pl.BlockSpec(memory_space=pl.ANY),
-        ]
-        + [pl.BlockSpec(memory_space=vmem)] * 4,
+        in_specs=[pl.BlockSpec(memory_space=pl.ANY)] * len(operands),
         out_specs=pl.BlockSpec(memory_space=vmem),
         scratch_shapes=[
+            vmem((8, 128), jnp.int32),
+            vmem((128, 128), jnp.int32),
+            vmem((TILES, DEPTH), jnp.int32),
+            vmem((16, 128), jnp.int32),
+            pltpu.SMEM((16, 128), jnp.int32),
+            pltpu.SMEM((NY,), jnp.int32),
+            pltpu.SMEM((NY,), jnp.int32),
+            vmem((9, OUT, CH + 1), bf16),
+            vmem((1, OUT), f32),
+            vmem((9, OUT, OUT), bf16),
+            vmem((1, OUT), f32),
+            dma((10,)),
             vmem((128,) + unit, bf16),
             vmem((128, ROWS, COLS), bf16),
             vmem((128, ROWS, COLS), bf16),
@@ -668,7 +703,7 @@
             vmem((16, OUT, TXD * COLS), bf16),
             vmem((NY, OUT, TXD * COLS), bf16),
             vmem((NY, OUT, TXD * COLS), bf16),
-            dma((5,)),
+            dma((4,)),
             dma((32,)),
             dma((32,)),
             dma((4, 8, 2)),
@@ -683,20 +718,22 @@
             dma((NY,)),
         ],
         compiler_params=pltpu.CompilerParams(
-            collective_id=0, has_side_effects=True, vmem_limit_bytes=48 << 20
+            collective_id=0, has_side_effects=True, vmem_limit_bytes=VMEM_BYTES
         ),
-    )(tab, payload, opacity, w1, b1, w2, b2)
+    )(*operands)
 
 
 def shards(
     payload, opacity, depth_order, footprints, panel_map,
     conv1_weight, conv1_bias, conv2_weight, conv2_bias,
 ):
-    tab = tables(footprints, depth_order, panel_map, lax.axis_index("gx"), lax.axis_index("gy"))
     shown = frame(
-        tab,
         payload.transpose(0, 2, 1, 3),
         opacity,
+        jnp.asarray(patterns()),
+        footprints,
+        depth_order,
+        panel_map,
         conv1_weight,
         conv1_bias[None],
         conv2_weight,

time: 78.2 us -> 67.5 us (0.86)
  local copies, waits for them, and re-layouts: 7.23 us -> 1.67 us
  other arithmetic: 4.79 us -> 0 us
    unnamed x13 -> x1, local copies, waits for them, and re-layouts: 6.98 us -> 1.67 us
    add x5 -> x0, other arithmetic: 2.88 us -> none  [the longest x1 0.79 us: tables(): (part * NY + depth_order % NY) * 6 + (tile // TXD - 1 + part) * TXD]
    reduce_sum x3 -> x0, other arithmetic: 1.11 us -> none  [the longest x1 0.74 us: tables(): jnp.sum(jnp.where(panel_map[:, None] == panels[None, :], panels[:, None],...]
where the time goes in v3:
time: 67.5 us; the launch traced here: 67.4 us
  Pallas kernels  65.7 us (97%)
  local copies, waits for them, and re-layouts  1.67 us (2%)
    pallas_call x1, Pallas kernels, frame(): pl.pallas_call(frame_kernel, name='frame', out_shape=jax.ShapeDtypeStruct...  65.7 us
    unnamed x1, local copies, waits for them, and re-layouts  1.67 us

profile of v3, /device:TPU:0, one launch (start us, length us, event | category | flops | bytes accessed | tf_op | source)
XLA Modules:
  0.0 67.4 jit_solution(1721737689059920922)
XLA Ops:
  0.0 65.7 %frame.1 = bf16[32,4096]{1,0:T(8,128)(2,1)} custom-call(bf16[128,35,4,128]{3,2,1,0:T(4,128)(2,1)} %bitcast.4, bf16[128,4,128]{2,1,0:T(4,128)(2,1)} %opa_h.1, s32[8,128]{1,0:T(8,128)} %constant.2.clone.rows_h, s32[128,128]{1,0:T(8,128)} %foot_h.1, s32[8,16]{1,0:T(8,128)} %order_h.1, s32[16]{0:T(128)} %panel_h.1, bf16[9,32,36]{2,1,0:T(8,128)(2,1)} %w1_h.1, ...), custom_call_target="tpu_custom_call" | custom-call | tf_op jit(solution)/shard_map/frame/pallas_call | solution.py:653
  65.7 1.7 %copy.12 = bf16[1,1,1,32,4096]{4,3,2,1,0:T(8,128)(2,1)} copy(bf16[1,1,1,32,4096]{4,3,2,1,0:T(8,128)(2,1)} %bitcast.5) | data formatting | bytes 524288

commit v4 on v3

--- a/solution.py
+++ b/solution.py
@@ -109,8 +109,8 @@
     pay_h, opa_h, rows_h, foot_h, order_h, panel_h, w1_h, b1_h, w2_h, b2_h, shown,
     rows, foot, order, tabv, tab, panel, inv, w1, b1, w2, b2, tsem,
     pay, opa, asend, abuf, tb, tsend, trecv, s1, r1, s2, acc, r2, s3, r3, s4, r4, ys, yr,
-    cov, stage, v1, pack, side, corner, band1, band2, h_acc, v2, v2_top, v2_low, o_acc, shaded, strips, got,
-    lsem, a_s, a_r, t_s, t_r, m_s, m_r, y_s, y_r, h_s, h_r, d_s, d_r,
+    cov, cov_side, cov_over, cov_under, stage, stage_y, v1, pack, rim, edge, band1, band2, h_acc, v2, v2_top, v2_low, o_acc, shaded, strips, got,
+    lsem, a_s, a_r, t_s, t_r, m_s, m_r, y_s, y_r, c_s, c_r, h_s, h_r, d_s, d_r,
 ):
     gx = lax.axis_index("gx")
     me = lax.axis_index("gy")
@@ -257,13 +257,18 @@
         0, DEPTH, through, tuple(jnp.ones((ROWS, COLS), jnp.float32) for _ in range(TILES))
     )
     for t in range(TILES):
-        cov[t] = 1.0 - last[t]
+        cov[t] = (1.0 - last[t]).astype(jnp.bfloat16)
 
     def fill(i, _):
-        tsend[i] = tb[tab[2 + i // 128, i % 128]]
-        return 0
-
-    lax.fori_loop(0, 192, fill, 0, unroll=8)
+        tsend[i] = tb[tab[2, i]]
+        return 0
+
+    def fill_rest(i, _):
+        tsend[128 + i] = tb[tab[3, i]]
+        return 0
+
+    lax.fori_loop(0, 128, fill, 0, unroll=8)
+    lax.fori_loop(0, 64, fill_rest, 0, unroll=8)
 
     def weight_range(q, k, back):
         g = q // 2
@@ -292,6 +297,33 @@
                 else:
                     weights[q, k, back] = weight_copy(q, k, back)
                     weights[q, k, back].start()
+    right = (me + 1) % NY
+    left = (me + NY - 1) % NY
+    first_row = pl.ds(0, TXD)
+    last_row = pl.ds((TYD - 1) * TXD, TXD)
+    covers = [
+        pltpu.make_async_remote_copy(
+            src_ref=src,
+            dst_ref=dst,
+            send_sem=c_s.at[n],
+            recv_sem=c_r.at[n],
+            device_id=(row, col),
+            device_id_type=MESH,
+        )
+        for n, (src, dst, row, col) in enumerate(
+            (
+                (cov, cov_side.at[0], gx, right),
+                (cov, cov_side.at[1], gx, left),
+                (cov.at[last_row], cov_over.at[0], up, right),
+                (cov.at[last_row], cov_over.at[1], up, left),
+                (cov.at[first_row], cov_under.at[0], down, right),
+                (cov.at[first_row], cov_under.at[1], down, left),
+                (cov.at[first_row], cov_under.at[2], down, me),
+            )
+        )
+    ]
+    for copy in covers:
+        copy.start()
     for n in range(2, 4):
         for q in range(4):
             raw[q][n].start()
@@ -343,7 +375,20 @@
 
     two = [[step_copy(s2, r2, q, lo, hi, 2, 4 + n) for n, (lo, hi) in enumerate(groups[1:])] for q in range(4)]
     three = [[step_copy(s3, r3, q, lo, hi, 3, 7 + n) for n, (lo, hi) in enumerate(groups[2:])] for q in range(4)]
-    four = [step_copy(s4, r4, q, 0, 1, 4, 9) for q in range(4)]
+
+    def last_copy(q, crossing):
+        size = 2 - q // 2 if crossing else 1 + q // 2
+        part = pl.ds(1 + q // 2 if crossing else 0, size)
+        return pltpu.make_async_remote_copy(
+            src_ref=s4.at[q, 0, part],
+            dst_ref=r4.at[q, 0, part],
+            send_sem=m_s.at[q, 9 + crossing],
+            recv_sem=m_r.at[q, 9 + crossing],
+            device_id=(gx, paired(me, MASKS[q][3])),
+            device_id_type=MESH,
+        )
+
+    four = [[last_copy(q, crossing) for crossing in range(2)] for q in range(4)]
 
     for q in range(4):
         wait_weights(q, 4, 8)
@@ -385,7 +430,8 @@
     for q in range(4):
         three[q][0].wait_recv()
         forward(s4, r3, q, 1, 0)
-        four[q].start()
+        four[q][1].start()
+        four[q][0].start()
     for q in range(4):
         three[q][1].wait_recv()
         keep(r3, q, 0)
@@ -402,15 +448,39 @@
         )
 
     cross = [cross_copy(q) for q in range(4)]
-    right = (me + 1) % NY
-    left = (me + NY - 1) % NY
+
+    def spread(ref, v):
+        for c in range(CH):
+            ref[pl.ds(c * ROWS, ROWS), :] = v[c]
 
     def place(jy, j, v):
-        lanes = pl.ds(j * COLS, COLS)
-        for c in range(CH):
-            stage[jy, j, pl.ds(c * ROWS, ROWS), :] = v[c]
-        stage[jy, j, pl.ds(CH * ROWS, ROWS), :] = cov[jy * TXD + j]
-        v1[jy + 1, :, lanes] = stage[jy, j].astype(jnp.bfloat16)
+        spread(stage.at[jy, j], v)
+        stage[jy, j, pl.ds(CH * ROWS, ROWS), :] = cov[jy * TXD + j].astype(jnp.float32)
+        v1[jy + 1, :, pl.ds(j * COLS, COLS)] = stage[jy, j].astype(jnp.bfloat16)
+
+    def final(q, e):
+        return acc[q, 0, e] + r4[q, 0, e].astype(jnp.float32)
+
+    for q in range(4):
+        g, j = q // 2, q % 2
+        four[q][1].wait_recv()
+        ys[q, 1] = final(q, 2).astype(jnp.bfloat16)
+        if g == 0:
+            ys[q, 0] = final(q, 1).astype(jnp.bfloat16)
+        cross[q].start()
+    for q in range(4):
+        g, j = q // 2, q % 2
+        spread(stage_y.at[1 + g, j], ys[q, 1].astype(jnp.float32))
+        if g == 0:
+            spread(stage_y.at[0, j], ys[q, 0].astype(jnp.float32))
+    for q in range(4):
+        g, j = q // 2, q % 2
+        four[q][0].wait_recv()
+        own = final(q, 0)
+        acc[q, 0, 0] = own
+        spread(stage.at[1 + g, j], own)
+        if g:
+            place(3, j, final(q, 1))
 
     def edge_copy(src, dst, n, row, col):
         return pltpu.make_async_remote_copy(
@@ -423,79 +493,92 @@
         )
 
     mine = pl.ds(0, TXD * COLS)
-    low = pl.ds(0, COLS)
-    high = pl.ds(COLS, COLS)
     edges = (
         edge_copy(v1.at[4, :, mine], v1.at[0, :, mine], 0, up, me),
-        edge_copy(v1.at[4, :, high], corner.at[0], 1, up, right),
-        edge_copy(v1.at[4, :, low], corner.at[1], 2, up, left),
-        edge_copy(v1.at[1, :, mine], v1.at[5, :, mine], 3, down, me),
-        edge_copy(v1.at[1, :, high], corner.at[2], 4, down, right),
-        edge_copy(v1.at[1, :, low], corner.at[3], 5, down, left),
-        edge_copy(pack.at[0], side.at[0], 6, gx, right),
-        edge_copy(pack.at[1], side.at[1], 7, gx, left),
+        edge_copy(pack.at[0, 0], rim.at[0, 0], 1, gx, right),
+        edge_copy(pack.at[0, 1], rim.at[0, 1], 2, gx, left),
+        edge_copy(pack.at[1, 0], rim.at[1, 0], 3, up, right),
+        edge_copy(pack.at[1, 1], rim.at[1, 1], 4, up, left),
     )
-
-    for q in range(4):
-        g, j = q // 2, q % 2
-        four[q].wait_recv()
-        first, mid, third = added(r4, q, 0)
-        ys[q, 1] = third.astype(jnp.bfloat16)
-        if g == 0:
-            ys[q, 0] = mid.astype(jnp.bfloat16)
-        cross[q].start()
-        acc[q, 0, 0] = first
-        if g:
-            place(3, j, mid)
-    for n in range(3):
-        edges[n].start()
+    edges[0].start()
+
+    lane = lax.broadcasted_iota(jnp.int32, (8, COLS), 1)
+    groups_of = DEEP1 // 8
+
+    def packed(ref, side):
+        total = jnp.zeros((8, COLS), jnp.float32)
+        for i in range(groups_of):
+            v = ref[pl.ds(8 * i, 8), :]
+            if i:
+                v = pltpu.roll(v, 4 * i, 1)
+            pair = (COLS // 2 - 1 + 2 * i) % (COLS // 2) if side == 0 else 2 * i
+            total = jnp.where((lane >> 1) == pair, v, total)
+        return total
+
+    for side in range(2):
+        j = 1 - side
+        for n, ref in enumerate((stage.at[1, j], stage.at[2, j], stage.at[3, j], stage_y.at[0, j])):
+            pack[0, side, pl.ds(8 * n, 8), :] = packed(ref, side)
+        for n, ref in enumerate((stage.at[3, j], stage_y.at[0, j], stage_y.at[1, j], stage_y.at[2, j])):
+            pack[1, side, pl.ds(8 * n, 8), :] = packed(ref, side)
+        edges[1 + side].start()
+        edges[3 + side].start()
+
+    for copy in covers:
+        copy.wait_recv()
+    for j in range(TXD):
+        stage_y[0, j, pl.ds(CH * ROWS, ROWS), :] = cov_under[2, j].astype(jnp.float32)
+        low = jnp.where(gx < NX - 1, stage_y[0, j], 0.0)
+        v1[5, :, pl.ds(j * COLS, COLS)] = low.astype(jnp.bfloat16)
     for q in range(4):
         g, j = q // 2, q % 2
         cross[q].wait_recv()
         if g == 0:
             place(0, j, yr[q, 0].astype(jnp.float32))
         place(1 + g, j, acc[q, 0, 0] + yr[q, 1].astype(jnp.float32))
-        if q == 1:
-            for n in range(3, 6):
-                edges[n].start()
-
-    lane = lax.broadcasted_iota(jnp.int32, (DEEP1, COLS), 1)
-    to_right = stage[0, 1]
-    to_left = stage[0, 0]
-    for jy in range(1, TYD):
-        spot = (lane // 2) == (COLS // 2 - 1 - jy)
-        to_right = jnp.where(spot, pltpu.roll(stage[jy, 1], COLS - 2 * jy, 1), to_right)
-        spot = (lane // 2) == jy
-        to_left = jnp.where(spot, pltpu.roll(stage[jy, 0], 2 * jy, 1), to_left)
-    pack[0] = to_right.astype(jnp.bfloat16)
-    pack[1] = to_left.astype(jnp.bfloat16)
-    edges[6].start()
-    edges[7].start()
     for copy in edges:
         copy.wait_recv()
 
-    on_right = jnp.logical_and(lane < COLS // 2, me < NY - 1)
-    on_left = jnp.logical_and(lane >= COLS // 2, me > 0)
     last_tile = pl.ds(2 * COLS, COLS)
-    zero = jnp.zeros((DEEP1, COLS), jnp.float32)
-    from_left = side[0].astype(jnp.float32)
-    from_right = side[1].astype(jnp.float32)
-    for jy in range(TYD):
-        r_part = pltpu.roll(from_right, COLS - 2 * jy, 1) if jy else from_right
-        l_part = pltpu.roll(from_left, 2 * jy, 1) if jy else from_left
-        rim = jnp.where(on_right, r_part, jnp.where(on_left, l_part, zero))
-        v1[jy + 1, :, last_tile] = rim.astype(jnp.bfloat16)
+    cover_lane = lax.broadcasted_iota(jnp.int32, (ROWS, COLS), 1)
+    has = (me > 0, me < NY - 1)
+    for blk in range(-1, TYD + 1):
+        total = None
+        for side in range(2):
+            part = None
+            if blk >= 1:
+                part = rim[0, side, pl.ds(8 * (blk - 1), 8), :]
+            if blk <= 2:
+                more = rim[1, side, pl.ds(8 * (blk + 1), 8), :]
+                part = more if part is None else part + more
+            part = jnp.where(has[side], part, 0.0)
+            total = part if total is None else total + part
+        if blk < 0:
+            sides = cov_over[0, 1], cov_over[1, 0]
+            inside = gx > 0
+        elif blk == TYD:
+            sides = cov_under[0, 1], cov_under[1, 0]
+            inside = gx < NX - 1
+        else:
+            sides = cov_side[0, blk * TXD + 1], cov_side[1, blk * TXD]
+            inside = None
+        covered = jnp.where(
+            cover_lane >= COLS // 2,
+            jnp.where(has[0], sides[0].astype(jnp.float32), 0.0),
+            jnp.where(has[1], sides[1].astype(jnp.float32), 0.0),
+        )
+        for i in range(groups_of):
+            edge[blk + 1, pl.ds(8 * i, 8), :] = pltpu.roll(total, COLS - 4 * i, 1) if i else total
+        edge[blk + 1, pl.ds(CH * ROWS, ROWS), :] = covered
+        value = edge[blk + 1]
+        if inside is not None:
+            value = jnp.where(inside, value, 0.0)
+        v1[blk + 1, :, last_tile] = value.astype(jnp.bfloat16)
     wide_zero = jnp.zeros((DEEP1, TXD * COLS), jnp.bfloat16)
-    for blk, base, inside in ((0, 0, gx > 0), (5, 2, gx < NX - 1)):
-        l_part = corner[base].astype(jnp.float32)
-        r_part = corner[base + 1].astype(jnp.float32)
-        rim = jnp.where(on_right, r_part, jnp.where(on_left, l_part, zero))
-        rim = jnp.where(inside, rim, zero)
-        v1[blk, :, last_tile] = rim.astype(jnp.bfloat16)
-
-        @pl.when(jnp.logical_not(inside))
-        def _(blk=blk):
-            v1[blk, :, mine] = wide_zero
+
+    @pl.when(gx == 0)
+    def _():
+        v1[0, :, mine] = wide_zero
 
     def product(band, rows, field):
         total = None
@@ -609,6 +692,8 @@
     lax.fori_loop(1, NY, strip_sent, 0)
     for copy in edges:
         copy.wait_send()
+    for copy in covers:
+        copy.wait_send()
 
     def alpha_sent(n, _):
         alpha_copy((me + n) % NY, 0).wait_send()
@@ -620,7 +705,7 @@
     for copy in weights.values():
         copy.wait_send()
     for q in range(4):
-        for copy in raw[q] + two[q] + three[q] + [four[q], cross[q]]:
+        for copy in raw[q] + two[q] + three[q] + four[q] + [cross[q]]:
             copy.wait_send()
 
 
@@ -687,12 +772,16 @@
             vmem((4, 1, 3) + unit, bf16),
             vmem((4, 2) + unit, bf16),
             vmem((4, 2) + unit, bf16),
-            vmem((TILES, ROWS, COLS), f32),
+            vmem((TILES, ROWS, COLS), bf16),
+            vmem((2, TILES, ROWS, COLS), bf16),
+            vmem((2, TXD, ROWS, COLS), bf16),
+            vmem((3, TXD, ROWS, COLS), bf16),
             vmem((TYD, TXD, DEEP1, COLS), f32),
+            vmem((3, TXD, DEEP1, COLS), f32),
             vmem((TYD + 2, DEEP1, WIDE), bf16),
-            vmem((2, DEEP1, COLS), bf16),
-            vmem((2, DEEP1, COLS), bf16),
-            vmem((4, DEEP1, COLS), bf16),
+            vmem((2, 2, 32, COLS), f32),
+            vmem((2, 2, 32, COLS), f32),
+            vmem((TYD + 2, DEEP1, COLS), f32),
             vmem((3, 6 * OUT, DEEP1), bf16),
             vmem((3, 6 * OUT, DEEP2), bf16),
             vmem((18, OUT, WIDE), f32),
@@ -708,12 +797,14 @@
             dma((32,)),
             dma((4, 8, 2)),
             dma((4, 8, 2)),
-            dma((4, 10)),
-            dma((4, 10)),
+            dma((4, 11)),
+            dma((4, 11)),
             dma((4,)),
             dma((4,)),
-            dma((8,)),
-            dma((8,)),
+            dma((7,)),
+            dma((7,)),
+            dma((5,)),
+            dma((5,)),
             dma((NY,)),
             dma((NY,)),
         ],

time: 67.5 us -> 64.6 us (0.957)
  Pallas kernels: 65.7 us -> 62.8 us
    pallas_call x1, Pallas kernels: 65.7 us -> 62.8 us  [frame(): pl.pallas_call(frame_kernel, name='frame', out_shape=jax.ShapeDtypeStruct...]
where the time goes in v4:
time: 64.6 us; the launch traced here: 64.5 us
  Pallas kernels  62.8 us (97%)
  local copies, waits for them, and re-layouts  1.67 us (3%)
    pallas_call x1, Pallas kernels, frame(): pl.pallas_call(frame_kernel, name='frame', out_shape=jax.ShapeDtypeStruct...  62.8 us
    unnamed x1, local copies, waits for them, and re-layouts  1.67 us

profile of v4, /device:TPU:0, one launch (start us, length us, event | category | flops | bytes accessed | tf_op | source)
XLA Modules:
  0.0 64.5 jit_solution(3943145928249616250)
XLA Ops:
  0.0 62.8 %frame.1 = bf16[32,4096]{1,0:T(8,128)(2,1)} custom-call(bf16[128,35,4,128]{3,2,1,0:T(4,128)(2,1)} %bitcast.4, bf16[128,4,128]{2,1,0:T(4,128)(2,1)} %opa_h.1, s32[8,128]{1,0:T(8,128)} %constant.2.clone.rows_h, s32[128,128]{1,0:T(8,128)} %foot_h.1, s32[8,16]{1,0:T(8,128)} %order_h.1, s32[16]{0:T(128)} %panel_h.1, bf16[9,32,36]{2,1,0:T(8,128)(2,1)} %w1_h.1, ...), custom_call_target="tpu_custom_call" | custom-call | tf_op jit(solution)/shard_map/frame/pallas_call | solution.py:738
  62.8 1.7 %copy.12 = bf16[1,1,1,32,4096]{4,3,2,1,0:T(8,128)(2,1)} copy(bf16[1,1,1,32,4096]{4,3,2,1,0:T(8,128)(2,1)} %bitcast.5) | data formatting | bytes 524288

commit v5 on v4

--- a/solution.py
+++ b/solution.py
@@ -26,6 +26,19 @@
 def kappa(q, k):
     m = MASKS[q]
     return (m[1] if k & 4 else 0) ^ (m[2] if k & 2 else 0) ^ (m[3] if k & 1 else 0)
+
+
+def hops(offset):
+    return sum(min(d, SIDE - d) for d in offset)
+
+
+OTHERS = sorted(
+    ((dx, dz) for dx in range(SIDE) for dz in range(SIDE) if dx or dz), key=hops, reverse=True
+)
+
+
+def shifted(c, offset):
+    return (c // SIDE + offset[0]) % SIDE * SIDE + (c % SIDE + offset[1]) % SIDE
 
 
 def flip4(p, d):
@@ -124,8 +137,8 @@
         )
     ]
     loads = []
-    for i in range(4):
-        part = pl.ds(32 * i, 32)
+    for i in range(8):
+        part = pl.ds(16 * i, 16)
         loads.append(pltpu.make_async_copy(pay_h.at[part], pay.at[part], lsem.at[i]))
     for load in early[:4] + loads + early[4:]:
         load.start()
@@ -184,12 +197,9 @@
             device_id_type=MESH,
         )
 
-    def alpha_start(n, _):
-        alpha_copy((me + n) % NY, 0).start()
-        alpha_copy((me + n) % NY, 1).start()
-        return 0
-
-    lax.fori_loop(1, NY, alpha_start, 0)
+    for offset in OTHERS:
+        alpha_copy(shifted(me, offset), 1).start()
+        alpha_copy(shifted(me, offset), 0).start()
     alpha_copy(me, 1).start()
 
     groups = ((4, 8), (2, 4), (1, 2), (0, 1))
@@ -260,11 +270,11 @@
         cov[t] = (1.0 - last[t]).astype(jnp.bfloat16)
 
     def fill(i, _):
-        tsend[i] = tb[tab[2, i]]
+        tsend[i] = tb[tab[2, i]].astype(jnp.bfloat16)
         return 0
 
     def fill_rest(i, _):
-        tsend[128 + i] = tb[tab[3, i]]
+        tsend[128 + i] = tb[tab[3, i]].astype(jnp.bfloat16)
         return 0
 
     lax.fori_loop(0, 128, fill, 0, unroll=8)
@@ -331,13 +341,14 @@
     def weighed(q, k):
         own = (q * 8 + k) * 2
         lead = (q * 8 + k) * 6
+        w = [trecv[lead + n].astype(jnp.float32)[None] for n in range(6)]
         own_f = pay[tab[1, own]].astype(jnp.float32)
         got_f = r1[q, k, 0].astype(jnp.float32)
-        mid = trecv[lead + 2][None] * own_f + trecv[lead + 3][None] * got_f
+        mid = w[2] * own_f + w[3] * got_f
         own_a = pay[tab[1, own + 1]].astype(jnp.float32)
         got_a = r1[q, k, 1].astype(jnp.float32)
-        first = trecv[lead][None] * own_a + trecv[lead + 1][None] * got_a
-        third = trecv[lead + 4][None] * own_a + trecv[lead + 5][None] * got_a
+        first = w[0] * own_a + w[1] * got_a
+        third = w[4] * own_a + w[5] * got_a
         return first, mid, third
 
     def merge_sent(q, lo, hi):
@@ -660,13 +671,10 @@
             device_id_type=MESH,
         )
 
-    def strip_start(n, _):
-        g = (me + n) % NY
+    for offset in OTHERS:
+        g = shifted(me, offset)
         strips[g] = shaded[inv[g]]
         strip_copy(g).start()
-        return 0
-
-    lax.fori_loop(1, NY, strip_start, 0)
     got[me] = shaded[inv[me]]
 
     def strip_wait(n, _):
@@ -759,8 +767,8 @@
             vmem((128, ROWS, COLS), bf16),
             vmem((192, ROWS, COLS), bf16),
             vmem((TILES * TSTEP, ROWS, COLS), f32),
-            vmem((192, ROWS, COLS), f32),
-            vmem((192, ROWS, COLS), f32),
+            vmem((192, ROWS, COLS), bf16),
+            vmem((192, ROWS, COLS), bf16),
             vmem((4, 8, 2) + unit, bf16),
             vmem((4, 8, 2) + unit, bf16),
             vmem((4, 4, 3) + unit, bf16),
@@ -792,7 +800,7 @@
             vmem((16, OUT, TXD * COLS), bf16),
             vmem((NY, OUT, TXD * COLS), bf16),
             vmem((NY, OUT, TXD * COLS), bf16),
-            dma((4,)),
+            dma((8,)),
             dma((32,)),
             dma((32,)),
             dma((4, 8, 2)),

time: 64.6 us -> 63.1 us (0.977)
  Pallas kernels: 62.8 us -> 61.3 us
    pallas_call x1, Pallas kernels: 62.8 us -> 61.3 us  [frame(): pl.pallas_call(frame_kernel, name='frame', out_shape=jax.ShapeDtypeStruct...]
where the time goes in v5:
time: 63.1 us; the launch traced here: 62.9 us
  Pallas kernels  61.3 us (97%)
  local copies, waits for them, and re-layouts  1.67 us (3%)
    pallas_call x1, Pallas kernels, frame(): pl.pallas_call(frame_kernel, name='frame', out_shape=jax.ShapeDtypeStruct...  61.3 us
    unnamed x1, local copies, waits for them, and re-layouts  1.67 us

profile of v5, /device:TPU:0, one launch (start us, length us, event | category | flops | bytes accessed | tf_op | source)
XLA Modules:
  0.0 62.9 jit_solution(15942594984656566333)
XLA Ops:
  0.0 61.3 %frame.1 = bf16[32,4096]{1,0:T(8,128)(2,1)} custom-call(bf16[128,35,4,128]{3,2,1,0:T(4,128)(2,1)} %bitcast.4, bf16[128,4,128]{2,1,0:T(4,128)(2,1)} %opa_h.1, s32[8,128]{1,0:T(8,128)} %constant.2.clone.rows_h, s32[128,128]{1,0:T(8,128)} %foot_h.1, s32[8,16]{1,0:T(8,128)} %order_h.1, s32[16]{0:T(128)} %panel_h.1, bf16[9,32,36]{2,1,0:T(8,128)(2,1)} %w1_h.1, ...), custom_call_target="tpu_custom_call" | custom-call | tf_op jit(solution)/shard_map/frame/pallas_call | solution.py:746
  61.3 1.7 %copy.12 = bf16[1,1,1,32,4096]{4,3,2,1,0:T(8,128)(2,1)} copy(bf16[1,1,1,32,4096]{4,3,2,1,0:T(8,128)(2,1)} %bitcast.5) | data formatting | bytes 524288

commit v6 on v5

--- a/solution.py
+++ b/solution.py
@@ -107,8 +107,7 @@
 
     tile = lax.broadcasted_iota(i32, (TILES, DEPTH), 0)
     part = jnp.minimum((gx - (listed >> 4)) & (NX - 1), 1)
-    spot = ((tile >> 1) - 1 + part) * TXD + (tile & 1)
-    out[8:16, 0:DEPTH] = jnp.maximum((part * NY + (listed & (NY - 1))) * 6 + spot, 0)
+    out[8:16, 0:DEPTH] = (part * NY + (listed & (NY - 1))) * TILES + tile
 
 
 OUT = 32
@@ -122,7 +121,7 @@
     pay_h, opa_h, rows_h, foot_h, order_h, panel_h, w1_h, b1_h, w2_h, b2_h, shown,
     rows, foot, order, tabv, tab, panel, inv, w1, b1, w2, b2, tsem,
     pay, opa, asend, abuf, tb, tsend, trecv, s1, r1, s2, acc, r2, s3, r3, s4, r4, ys, yr,
-    cov, cov_side, cov_over, cov_under, stage, stage_y, v1, pack, rim, edge, band1, band2, h_acc, v2, v2_top, v2_low, o_acc, shaded, strips, got,
+    cov, cov_side, cov_over, cov_under, stage, stage_y, v1, pack, rim, edge, band1, band2, h_acc, v2, v2_top, v2_low, o_acc, shaded, strips,
     lsem, a_s, a_r, t_s, t_r, m_s, m_r, y_s, y_r, c_s, c_r, h_s, h_r, d_s, d_r,
 ):
     gx = lax.axis_index("gx")
@@ -170,8 +169,8 @@
         return 0
 
     lax.fori_loop(0, 128, pack_alpha, 0, unroll=8)
-    for e in range(6):
-        abuf[me * 6 + e] = asend[me * TILES + 2 + e]
+    for e in range(TILES):
+        abuf[me * TILES + e] = asend[me * TILES + e]
     for load in loads:
         load.wait()
 
@@ -187,20 +186,27 @@
         pack_raw(q, 2, 8)
     pl.semaphore_wait(barrier, 47)
 
-    def alpha_copy(i, back):
+    def alpha_copy(i):
         return pltpu.make_async_remote_copy(
-            src_ref=asend.at[pl.ds(i * TILES + 2 - 2 * back, 6)],
-            dst_ref=abuf.at[pl.ds((back * NY + me) * 6, 6)],
-            send_sem=a_s.at[back * NY + i],
-            recv_sem=a_r.at[back * NY + me],
-            device_id=(up if back else gx, i),
-            device_id_type=MESH,
-        )
+            src_ref=asend.at[pl.ds(i * TILES, TILES)],
+            dst_ref=abuf.at[pl.ds(me * TILES, TILES)],
+            send_sem=a_s.at[i],
+            recv_sem=a_r.at[me],
+            device_id=(gx, i),
+            device_id_type=MESH,
+        )
+
+    alpha_on = pltpu.make_async_remote_copy(
+        src_ref=abuf.at[pl.ds(0, 128)],
+        dst_ref=abuf.at[pl.ds(128, 128)],
+        send_sem=a_s.at[NY],
+        recv_sem=a_r.at[NY],
+        device_id=(up, me),
+        device_id_type=MESH,
+    )
 
     for offset in OTHERS:
-        alpha_copy(shifted(me, offset), 1).start()
-        alpha_copy(shifted(me, offset), 0).start()
-    alpha_copy(me, 1).start()
+        alpha_copy(shifted(me, offset)).start()
 
     groups = ((4, 8), (2, 4), (1, 2), (0, 1))
 
@@ -238,19 +244,19 @@
 
     def alpha_wait(n, _):
         col = (me + n) % NY
-        for back in range(2):
-            pltpu.make_async_remote_copy(
-                src_ref=asend.at[pl.ds(0, 6)],
-                dst_ref=abuf.at[pl.ds((back * NY + col) * 6, 6)],
-                send_sem=a_s.at[back * NY + col],
-                recv_sem=a_r.at[back * NY + col],
-                device_id=(gx, col),
-                device_id_type=MESH,
-            ).wait_recv()
+        pltpu.make_async_remote_copy(
+            src_ref=asend.at[pl.ds(0, TILES)],
+            dst_ref=abuf.at[pl.ds(col * TILES, TILES)],
+            send_sem=a_s.at[col],
+            recv_sem=a_r.at[col],
+            device_id=(gx, col),
+            device_id_type=MESH,
+        ).wait_recv()
         return 0
 
     lax.fori_loop(1, NY, alpha_wait, 0)
-    alpha_copy(me, 1).wait_recv()
+    alpha_on.start()
+    alpha_on.wait_recv()
 
     for t in range(TILES):
         tb[t * TSTEP + DEPTH + 1] = jnp.zeros((ROWS, COLS), jnp.float32)
@@ -661,10 +667,14 @@
             value = value + tail
         shaded[n] = value.astype(jnp.bfloat16)
 
+    def window(col):
+        start = pl.multiple_of(col * (TXD * COLS), TXD * COLS)
+        return shown.at[:, pl.ds(start, TXD * COLS)]
+
     def strip_copy(g):
         return pltpu.make_async_remote_copy(
             src_ref=strips.at[g],
-            dst_ref=got.at[me],
+            dst_ref=window(me),
             send_sem=d_s.at[g],
             recv_sem=d_r.at[me],
             device_id=(gx, g),
@@ -675,13 +685,15 @@
         g = shifted(me, offset)
         strips[g] = shaded[inv[g]]
         strip_copy(g).start()
-    got[me] = shaded[inv[me]]
+    strips[me] = shaded[inv[me]]
+    own_strip = pltpu.make_async_copy(strips.at[me], window(me), tsem.at[10])
+    own_strip.start()
 
     def strip_wait(n, _):
         col = (me + n) % NY
         pltpu.make_async_remote_copy(
             src_ref=strips.at[col],
-            dst_ref=got.at[col],
+            dst_ref=window(col),
             send_sem=d_s.at[col],
             recv_sem=d_r.at[col],
             device_id=(gx, col),
@@ -689,32 +701,29 @@
         ).wait_recv()
         return 0
 
-    lax.fori_loop(1, NY, strip_wait, 0)
-    for col in range(NY):
-        shown[:, pl.ds(col * TXD * COLS, TXD * COLS)] = got[col]
-
     def strip_sent(n, _):
         strip_copy((me + n) % NY).wait_send()
         return 0
 
-    lax.fori_loop(1, NY, strip_sent, 0)
     for copy in edges:
         copy.wait_send()
     for copy in covers:
         copy.wait_send()
 
     def alpha_sent(n, _):
-        alpha_copy((me + n) % NY, 0).wait_send()
-        alpha_copy((me + n) % NY, 1).wait_send()
+        alpha_copy((me + n) % NY).wait_send()
         return 0
 
     lax.fori_loop(1, NY, alpha_sent, 0)
-    alpha_copy(me, 1).wait_send()
+    alpha_on.wait_send()
     for copy in weights.values():
         copy.wait_send()
     for q in range(4):
         for copy in raw[q] + two[q] + three[q] + four[q] + [cross[q]]:
             copy.wait_send()
+    lax.fori_loop(1, NY, strip_sent, 0)
+    own_strip.wait()
+    lax.fori_loop(1, NY, strip_wait, 0)
 
 
 def spread_weights(w1, w2, band1, band2):
@@ -748,7 +757,7 @@
         name="frame",
         out_shape=jax.ShapeDtypeStruct((OUT, NY * TXD * COLS), bf16),
         in_specs=[pl.BlockSpec(memory_space=pl.ANY)] * len(operands),
-        out_specs=pl.BlockSpec(memory_space=vmem),
+        out_specs=pl.BlockSpec(memory_space=pl.ANY),
         scratch_shapes=[
             vmem((8, 128), jnp.int32),
             vmem((128, 128), jnp.int32),
@@ -761,11 +770,11 @@
             vmem((1, OUT), f32),
             vmem((9, OUT, OUT), bf16),
             vmem((1, OUT), f32),
-            dma((10,)),
+            dma((11,)),
             vmem((128,) + unit, bf16),
             vmem((128, ROWS, COLS), bf16),
             vmem((128, ROWS, COLS), bf16),
-            vmem((192, ROWS, COLS), bf16),
+            vmem((256, ROWS, COLS), bf16),
             vmem((TILES * TSTEP, ROWS, COLS), f32),
             vmem((192, ROWS, COLS), bf16),
             vmem((192, ROWS, COLS), bf16),
@@ -799,10 +808,9 @@
             vmem((16, OUT, TXD * COLS), f32),
             vmem((16, OUT, TXD * COLS), bf16),
             vmem((NY, OUT, TXD * COLS), bf16),
-            vmem((NY, OUT, TXD * COLS), bf16),
             dma((8,)),
-            dma((32,)),
-            dma((32,)),
+            dma((NY + 1,)),
+            dma((NY + 1,)),
             dma((4, 8, 2)),
             dma((4, 8, 2)),
             dma((4, 11)),

time: 63.1 us -> 61.1 us (0.968)
  Pallas kernels: 61.3 us -> 59.3 us
    pallas_call x1, Pallas kernels: 61.3 us -> 59.3 us  [frame(): pl.pallas_call(frame_kernel, name='frame', out_shape=jax.ShapeDtypeStruct...]
where the time goes in v6:
time: 61.1 us; the launch traced here: 61 us
  Pallas kernels  59.3 us (97%)
  local copies, waits for them, and re-layouts  1.67 us (3%)
    pallas_call x1, Pallas kernels, frame(): pl.pallas_call(frame_kernel, name='frame', out_shape=jax.ShapeDtypeStruct...  59.3 us
    unnamed x1, local copies, waits for them, and re-layouts  1.67 us

profile of v6, /device:TPU:0, one launch (start us, length us, event | category | flops | bytes accessed | tf_op | source)
XLA Modules:
  0.0 61.0 jit_solution(10717023471127399037)
XLA Ops:
  0.0 59.3 %frame.1 = bf16[32,4096]{1,0:T(8,128)(2,1)} custom-call(bf16[128,35,4,128]{3,2,1,0:T(4,128)(2,1)} %bitcast.4, bf16[128,4,128]{2,1,0:T(4,128)(2,1)} %opa_h.1, s32[8,128]{1,0:T(8,128)} %constant.2.clone.rows_h, s32[128,128]{1,0:T(8,128)} %foot_h.1, s32[8,16]{1,0:T(8,128)} %order_h.1, s32[16]{0:T(128)} %panel_h.1, bf16[9,32,36]{2,1,0:T(8,128)(2,1)} %w1_h.1, ...), custom_call_target="tpu_custom_call" | custom-call | tf_op jit(solution)/shard_map/frame/pallas_call | solution.py:755
  59.3 1.7 %copy.12 = bf16[1,1,1,32,4096]{4,3,2,1,0:T(8,128)(2,1)} copy(bf16[1,1,1,32,4096]{4,3,2,1,0:T(8,128)(2,1)} %bitcast.5) | data formatting | bytes 524288

commit v7 on v6

--- a/solution.py
+++ b/solution.py
@@ -122,12 +122,14 @@
     rows, foot, order, tabv, tab, panel, inv, w1, b1, w2, b2, tsem,
     pay, opa, asend, abuf, tb, tsend, trecv, s1, r1, s2, acc, r2, s3, r3, s4, r4, ys, yr,
     cov, cov_side, cov_over, cov_under, stage, stage_y, v1, pack, rim, edge, band1, band2, h_acc, v2, v2_top, v2_low, o_acc, shaded, strips,
-    lsem, a_s, a_r, t_s, t_r, m_s, m_r, y_s, y_r, c_s, c_r, h_s, h_r, d_s, d_r,
+    lsem, a_s, a_r, t_s, t_r, m_s, m_r, y_s, y_r, c_sem, h_s, h_r, d_sem,
 ):
     gx = lax.axis_index("gx")
     me = lax.axis_index("gy")
     up = (gx + 1) % NX
     down = (gx + NX - 1) % NX
+    right = (me + 1) % NY
+    left = (me + NY - 1) % NY
     early = [
         pltpu.make_async_copy(src, dst, tsem.at[n])
         for n, (src, dst) in enumerate(
@@ -138,7 +140,7 @@
     loads = []
     for i in range(8):
         part = pl.ds(16 * i, 16)
-        loads.append(pltpu.make_async_copy(pay_h.at[part], pay.at[part], lsem.at[i]))
+        loads.append(pltpu.make_async_copy(pay_h.at[part], pay.at[part], lsem))
     for load in early[:4] + loads + early[4:]:
         load.start()
 
@@ -171,8 +173,7 @@
     lax.fori_loop(0, 128, pack_alpha, 0, unroll=8)
     for e in range(TILES):
         abuf[me * TILES + e] = asend[me * TILES + e]
-    for load in loads:
-        load.wait()
+    pltpu.make_async_copy(pay_h, pay, lsem).wait()
 
     def pack_raw(q, lo, hi):
         def body(k, _):
@@ -190,8 +191,8 @@
         return pltpu.make_async_remote_copy(
             src_ref=asend.at[pl.ds(i * TILES, TILES)],
             dst_ref=abuf.at[pl.ds(me * TILES, TILES)],
-            send_sem=a_s.at[i],
-            recv_sem=a_r.at[me],
+            send_sem=a_s.at[0],
+            recv_sem=a_r.at[0],
             device_id=(gx, i),
             device_id_type=MESH,
         )
@@ -199,8 +200,8 @@
     alpha_on = pltpu.make_async_remote_copy(
         src_ref=abuf.at[pl.ds(0, 128)],
         dst_ref=abuf.at[pl.ds(128, 128)],
-        send_sem=a_s.at[NY],
-        recv_sem=a_r.at[NY],
+        send_sem=a_s.at[1],
+        recv_sem=a_r.at[1],
         device_id=(up, me),
         device_id_type=MESH,
     )
@@ -216,8 +217,8 @@
         return pltpu.make_async_remote_copy(
             src_ref=s1.at[q, part],
             dst_ref=r1.at[q, part],
-            send_sem=m_s.at[q, n],
-            recv_sem=m_r.at[q, n],
+            send_sem=m_s.at[0],
+            recv_sem=m_r.at[q, 0 if n == 0 else 1],
             device_id=(gx, paired(me, MASKS[q][0])),
             device_id_type=MESH,
         )
@@ -242,19 +243,16 @@
 
     spread_weights(w1, w2, band1, band2)
 
-    def alpha_wait(n, _):
-        col = (me + n) % NY
-        pltpu.make_async_remote_copy(
-            src_ref=asend.at[pl.ds(0, TILES)],
-            dst_ref=abuf.at[pl.ds(col * TILES, TILES)],
-            send_sem=a_s.at[col],
-            recv_sem=a_r.at[col],
-            device_id=(gx, col),
-            device_id_type=MESH,
-        ).wait_recv()
-        return 0
-
-    lax.fori_loop(1, NY, alpha_wait, 0)
+    others = pl.ds(0, (NY - 1) * TILES)
+    alphas = pltpu.make_async_remote_copy(
+        src_ref=asend.at[others],
+        dst_ref=abuf.at[others],
+        send_sem=a_s.at[0],
+        recv_sem=a_r.at[0],
+        device_id=(gx, right),
+        device_id_type=MESH,
+    )
+    alphas.wait_recv()
     alpha_on.start()
     alpha_on.wait_recv()
 
@@ -296,13 +294,12 @@
         return pltpu.make_async_remote_copy(
             src_ref=tsend.at[part],
             dst_ref=trecv.at[part],
-            send_sem=t_s.at[q, k, back],
-            recv_sem=t_r.at[q, k, back],
+            send_sem=t_s,
+            recv_sem=t_r.at[1 if k >= 4 else 0],
             device_id=(down if back else gx, paired(me, kappa(q, k))),
             device_id_type=MESH,
         )
 
-    weights = {}
     for k in (7, 6, 5, 4, 3, 2, 1, 0):
         for q in range(4):
             for back in range(2):
@@ -311,22 +308,31 @@
                     for e in range(4 if g else 2):
                         trecv[q * 48 + e] = tsend[q * 48 + e]
                 else:
-                    weights[q, k, back] = weight_copy(q, k, back)
-                    weights[q, k, back].start()
-    right = (me + 1) % NY
-    left = (me + NY - 1) % NY
+                    weight_copy(q, k, back).start()
+
+    def weight_group(size, sem):
+        part = pl.ds(0, size)
+        return pltpu.make_async_remote_copy(
+            src_ref=tsend.at[part],
+            dst_ref=trecv.at[part],
+            send_sem=t_s,
+            recv_sem=t_r.at[sem],
+            device_id=(gx, right),
+            device_id_type=MESH,
+        )
+
     first_row = pl.ds(0, TXD)
     last_row = pl.ds((TYD - 1) * TXD, TXD)
     covers = [
         pltpu.make_async_remote_copy(
             src_ref=src,
             dst_ref=dst,
-            send_sem=c_s.at[n],
-            recv_sem=c_r.at[n],
+            send_sem=c_sem.at[0],
+            recv_sem=c_sem.at[1],
             device_id=(row, col),
             device_id_type=MESH,
         )
-        for n, (src, dst, row, col) in enumerate(
+        for src, dst, row, col in (
             (
                 (cov, cov_side.at[0], gx, right),
                 (cov, cov_side.at[1], gx, left),
@@ -340,6 +346,15 @@
     ]
     for copy in covers:
         copy.start()
+    covered_part = pl.ds(0, 2 * TILES + 5 * TXD)
+    all_covers = pltpu.make_async_remote_copy(
+        src_ref=asend.at[covered_part],
+        dst_ref=abuf.at[covered_part],
+        send_sem=c_sem.at[0],
+        recv_sem=c_sem.at[1],
+        device_id=(gx, right),
+        device_id_type=MESH,
+    )
     for n in range(2, 4):
         for q in range(4):
             raw[q][n].start()
@@ -378,20 +393,24 @@
         return pltpu.make_async_remote_copy(
             src_ref=src.at[q, part],
             dst_ref=dst.at[q, part],
-            send_sem=m_s.at[q, sem],
+            send_sem=m_s.at[step - 1],
             recv_sem=m_r.at[q, sem],
             device_id=(gx, paired(me, MASKS[q][step - 1])),
             device_id_type=MESH,
         )
 
-    def wait_weights(q, lo, hi):
-        for k in range(lo, hi):
-            for back in range(2):
-                if (q, k, back) in weights:
-                    weights[q, k, back].wait_recv()
-
-    two = [[step_copy(s2, r2, q, lo, hi, 2, 4 + n) for n, (lo, hi) in enumerate(groups[1:])] for q in range(4)]
-    three = [[step_copy(s3, r3, q, lo, hi, 3, 7 + n) for n, (lo, hi) in enumerate(groups[2:])] for q in range(4)]
+    def whole(src, dst, part, send, recv):
+        return pltpu.make_async_remote_copy(
+            src_ref=src.at[part],
+            dst_ref=dst.at[part],
+            send_sem=send,
+            recv_sem=recv,
+            device_id=(gx, right),
+            device_id_type=MESH,
+        )
+
+    two = [[step_copy(s2, r2, q, lo, hi, 2, 2 + n) for n, (lo, hi) in enumerate(groups[1:])] for q in range(4)]
+    three = [[step_copy(s3, r3, q, lo, hi, 3, 5 + n) for n, (lo, hi) in enumerate(groups[2:])] for q in range(4)]
 
     def last_copy(q, crossing):
         size = 2 - q // 2 if crossing else 1 + q // 2
@@ -399,16 +418,16 @@
         return pltpu.make_async_remote_copy(
             src_ref=s4.at[q, 0, part],
             dst_ref=r4.at[q, 0, part],
-            send_sem=m_s.at[q, 9 + crossing],
-            recv_sem=m_r.at[q, 9 + crossing],
+            send_sem=m_s.at[3],
+            recv_sem=m_r.at[q, 7 + crossing],
             device_id=(gx, paired(me, MASKS[q][3])),
             device_id_type=MESH,
         )
 
     four = [[last_copy(q, crossing) for crossing in range(2)] for q in range(4)]
 
-    for q in range(4):
-        wait_weights(q, 4, 8)
+    weight_group(96, 1).wait_recv()
+    for q in range(4):
         raw[q][0].wait_recv()
         merge_sent(q, 6, 8)
         two[q][0].start()
@@ -416,10 +435,10 @@
         merge_sent(q, 4, 6)
         two[q][1].start()
         two[q][2].start()
-    for q in range(4):
-        wait_weights(q, 0, 4)
-        for n in range(1, 4):
-            raw[q][n].wait_recv()
+    weight_group(84, 0).wait_recv()
+    for q in range(4):
+        half = (q, pl.ds(0, 4))
+        whole(s1, r1, half, m_s.at[0], m_r.at[q, 1]).wait_recv()
         merge_kept(q, 0, 4)
 
     def added(src, q, k):
@@ -458,7 +477,7 @@
         return pltpu.make_async_remote_copy(
             src_ref=ys.at[q, part],
             dst_ref=yr.at[q, part],
-            send_sem=y_s.at[q],
+            send_sem=y_s,
             recv_sem=y_r.at[q],
             device_id=(up, me),
             device_id_type=MESH,
@@ -500,6 +519,7 @@
             place(3, j, final(q, 1))
 
     def edge_copy(src, dst, n, row, col):
+        n = min(n, 1)
         return pltpu.make_async_remote_copy(
             src_ref=src,
             dst_ref=dst,
@@ -541,8 +561,7 @@
         edges[1 + side].start()
         edges[3 + side].start()
 
-    for copy in covers:
-        copy.wait_recv()
+    all_covers.wait_recv()
     for j in range(TXD):
         stage_y[0, j, pl.ds(CH * ROWS, ROWS), :] = cov_under[2, j].astype(jnp.float32)
         low = jnp.where(gx < NX - 1, stage_y[0, j], 0.0)
@@ -553,8 +572,9 @@
         if g == 0:
             place(0, j, yr[q, 0].astype(jnp.float32))
         place(1 + g, j, acc[q, 0, 0] + yr[q, 1].astype(jnp.float32))
-    for copy in edges:
-        copy.wait_recv()
+    rims = whole(pack, rim, pl.ds(0, 2), h_s.at[1], h_r.at[1])
+    edges[0].wait_recv()
+    rims.wait_recv()
 
     last_tile = pl.ds(2 * COLS, COLS)
     cover_lane = lax.broadcasted_iota(jnp.int32, (ROWS, COLS), 1)
@@ -675,8 +695,8 @@
         return pltpu.make_async_remote_copy(
             src_ref=strips.at[g],
             dst_ref=window(me),
-            send_sem=d_s.at[g],
-            recv_sem=d_r.at[me],
+            send_sem=d_sem.at[0],
+            recv_sem=d_sem.at[1],
             device_id=(gx, g),
             device_id_type=MESH,
         )
@@ -685,45 +705,31 @@
         g = shifted(me, offset)
         strips[g] = shaded[inv[g]]
         strip_copy(g).start()
-    strips[me] = shaded[inv[me]]
-    own_strip = pltpu.make_async_copy(strips.at[me], window(me), tsem.at[10])
-    own_strip.start()
-
-    def strip_wait(n, _):
-        col = (me + n) % NY
-        pltpu.make_async_remote_copy(
-            src_ref=strips.at[col],
-            dst_ref=window(col),
-            send_sem=d_s.at[col],
-            recv_sem=d_r.at[col],
-            device_id=(gx, col),
-            device_id_type=MESH,
-        ).wait_recv()
-        return 0
-
-    def strip_sent(n, _):
-        strip_copy((me + n) % NY).wait_send()
-        return 0
-
-    for copy in edges:
-        copy.wait_send()
-    for copy in covers:
-        copy.wait_send()
-
-    def alpha_sent(n, _):
-        alpha_copy((me + n) % NY).wait_send()
-        return 0
-
-    lax.fori_loop(1, NY, alpha_sent, 0)
+    start = pl.multiple_of(me * (TXD * COLS), TXD * COLS)
+    shown[:, pl.ds(start, TXD * COLS)] = shaded[inv[me]]
+
+    edges[0].wait_send()
+    rims.wait_send()
+    all_covers.wait_send()
+
+    alphas.wait_send()
     alpha_on.wait_send()
-    for copy in weights.values():
-        copy.wait_send()
-    for q in range(4):
-        for copy in raw[q] + two[q] + three[q] + four[q] + [cross[q]]:
-            copy.wait_send()
-    lax.fori_loop(1, NY, strip_sent, 0)
-    own_strip.wait()
-    lax.fori_loop(1, NY, strip_wait, 0)
+    weight_group(180, 0).wait_send()
+    every_q = pl.ds(0, 4)
+    for n, (src, dst) in enumerate(((s1, r1), (s2, r2), (s3, r3), (s4, r4))):
+        whole(src, dst, every_q, m_s.at[n], m_r.at[0, 0]).wait_send()
+    whole(ys, yr, pl.ds(0, 3), y_s, y_r.at[0]).wait_send()
+    parts = pl.ds(0, NY - 1)
+    all_strips = pltpu.make_async_remote_copy(
+        src_ref=strips.at[parts],
+        dst_ref=shaded.at[parts],
+        send_sem=d_sem.at[0],
+        recv_sem=d_sem.at[1],
+        device_id=(gx, right),
+        device_id_type=MESH,
+    )
+    all_strips.wait_send()
+    all_strips.wait_recv()
 
 
 def spread_weights(w1, w2, band1, band2):
@@ -757,7 +763,7 @@
         name="frame",
         out_shape=jax.ShapeDtypeStruct((OUT, NY * TXD * COLS), bf16),
         in_specs=[pl.BlockSpec(memory_space=pl.ANY)] * len(operands),
-        out_specs=pl.BlockSpec(memory_space=pl.ANY),
+        out_specs=pl.BlockSpec(memory_space=vmem),
         scratch_shapes=[
             vmem((8, 128), jnp.int32),
             vmem((128, 128), jnp.int32),
@@ -770,7 +776,7 @@
             vmem((1, OUT), f32),
             vmem((9, OUT, OUT), bf16),
             vmem((1, OUT), f32),
-            dma((11,)),
+            dma((10,)),
             vmem((128,) + unit, bf16),
             vmem((128, ROWS, COLS), bf16),
             vmem((128, ROWS, COLS), bf16),
@@ -808,21 +814,19 @@
             vmem((16, OUT, TXD * COLS), f32),
             vmem((16, OUT, TXD * COLS), bf16),
             vmem((NY, OUT, TXD * COLS), bf16),
-            dma((8,)),
-            dma((NY + 1,)),
-            dma((NY + 1,)),
-            dma((4, 8, 2)),
-            dma((4, 8, 2)),
-            dma((4, 11)),
-            dma((4, 11)),
+            dma(()),
+            dma((2,)),
+            dma((2,)),
+            dma(()),
+            dma((2,)),
             dma((4,)),
+            dma((4, 9)),
+            dma(()),
             dma((4,)),
-            dma((7,)),
-            dma((7,)),
-            dma((5,)),
-            dma((5,)),
-            dma((NY,)),
-            dma((NY,)),
+            dma((2,)),
+            dma((2,)),
+            dma((2,)),
+            dma((2,)),
         ],
         compiler_params=pltpu.CompilerParams(
             collective_id=0, has_side_effects=True, vmem_limit_bytes=VMEM_BYTES

time: 61.1 us -> 59.2 us (0.969)
  Pallas kernels: 59.3 us -> 57.4 us
    pallas_call x1, Pallas kernels: 59.3 us -> 57.4 us  [frame(): pl.pallas_call(frame_kernel, name='frame', out_shape=jax.ShapeDtypeStruct...]
where the time goes in v7:
time: 59.2 us; the launch traced here: 59.1 us
  Pallas kernels  57.4 us (97%)
  local copies, waits for them, and re-layouts  1.67 us (3%)
    pallas_call x1, Pallas kernels, frame(): pl.pallas_call(frame_kernel, name='frame', out_shape=jax.ShapeDtypeStruct...  57.4 us
    unnamed x1, local copies, waits for them, and re-layouts  1.67 us

profile of v7, /device:TPU:0, one launch (start us, length us, event | category | flops | bytes accessed | tf_op | source)
XLA Modules:
  0.0 59.1 jit_solution(14038122775924578585)
XLA Ops:
  0.0 57.4 %frame.1 = bf16[32,4096]{1,0:T(8,128)(2,1)} custom-call(bf16[128,35,4,128]{3,2,1,0:T(4,128)(2,1)} %bitcast.4, bf16[128,4,128]{2,1,0:T(4,128)(2,1)} %opa_h.1, s32[8,128]{1,0:T(8,128)} %constant.2.clone.rows_h, s32[128,128]{1,0:T(8,128)} %foot_h.1, s32[8,16]{1,0:T(8,128)} %order_h.1, s32[16]{0:T(128)} %panel_h.1, bf16[9,32,36]{2,1,0:T(8,128)(2,1)} %w1_h.1, ...), custom_call_target="tpu_custom_call" | custom-call | tf_op jit(solution)/shard_map/frame/pallas_call | solution.py:761
  57.4 1.7 %copy.12 = bf16[1,1,1,32,4096]{4,3,2,1,0:T(8,128)(2,1)} copy(bf16[1,1,1,32,4096]{4,3,2,1,0:T(8,128)(2,1)} %bitcast.5) | data formatting | bytes 524288

commit v8 on v7

--- a/solution.py
+++ b/solution.py
@@ -761,7 +761,7 @@
     return pl.pallas_call(
         frame_kernel,
         name="frame",
-        out_shape=jax.ShapeDtypeStruct((OUT, NY * TXD * COLS), bf16),
+        out_shape=vmem((OUT, NY * TXD * COLS), bf16),
         in_specs=[pl.BlockSpec(memory_space=pl.ANY)] * len(operands),
         out_specs=pl.BlockSpec(memory_space=vmem),
         scratch_shapes=[

time: 59.2 us -> 57.5 us (0.971)
  local copies, waits for them, and re-layouts: 1.67 us -> 0.71 us
  Pallas kernels: 57.4 us -> 56.7 us
    unnamed x1, local copies, waits for them, and re-layouts: 1.67 us -> 0.71 us
    pallas_call x1, Pallas kernels: 57.4 us -> 56.7 us  [frame(): pl.pallas_call(frame_kernel, name='frame', out_shape=vmem((OUT, NY * TXD...]
where the time goes in v8:
time: 57.5 us; the launch traced here: 57.4 us
  Pallas kernels  56.7 us (99%)
  local copies, waits for them, and re-layouts  0.71 us (1%)
    pallas_call x1, Pallas kernels, frame(): pl.pallas_call(frame_kernel, name='frame', out_shape=vmem((OUT, NY * TXD...  56.7 us

profile of v8, /device:TPU:0, one launch (start us, length us, event | category | flops | bytes accessed | tf_op | source)
XLA Modules:
  0.0 57.4 jit_solution(15933833106892135940)
XLA Ops:
  0.0 56.7 %frame.1 = bf16[32,4096]{1,0:T(8,128)(2,1)S(1)} custom-call(bf16[128,35,4,128]{3,2,1,0:T(4,128)(2,1)} %bitcast.5, bf16[128,4,128]{2,1,0:T(4,128)(2,1)} %opa_h.1, s32[8,128]{1,0:T(8,128)} %constant.2.clone.rows_h, s32[128,128]{1,0:T(8,128)} %foot_h.1, s32[8,16]{1,0:T(8,128)} %order_h.1, s32[16]{0:T(128)} %panel_h.1, bf16[9,32,36]{2,1,0:T(8,128)(2,1)} %w1_h.1, ...), custom_call_target="tpu_custom_call" | custom-call | tf_op jit(solution)/shard_map/frame/pallas_call | solution.py:761
  56.7 0.7 %copy.12 = bf16[1,1,1,32,4096]{4,3,2,1,0:T(8,128)(2,1)} copy(bf16[1,1,1,32,4096]{4,3,2,1,0:T(8,128)(2,1)S(1)} %bitcast.4) | data formatting | bytes 524288

commit v9 on v8

--- a/solution.py
+++ b/solution.py
@@ -111,17 +111,17 @@
 
 
 OUT = 32
+GROUP = 4
 VMEM_BYTES = 62 << 20
 WIDE = 3 * COLS
 DEEP1 = (CH + 1) * ROWS
-DEEP2 = OUT * ROWS
 
 
 def frame_kernel(
     pay_h, opa_h, rows_h, foot_h, order_h, panel_h, w1_h, b1_h, w2_h, b2_h, shown,
     rows, foot, order, tabv, tab, panel, inv, w1, b1, w2, b2, tsem,
     pay, opa, asend, abuf, tb, tsend, trecv, s1, r1, s2, acc, r2, s3, r3, s4, r4, ys, yr,
-    cov, cov_side, cov_over, cov_under, stage, stage_y, v1, pack, rim, edge, band1, band2, h_acc, v2, v2_top, v2_low, o_acc, shaded, strips,
+    cov, cov_side, cov_over, cov_under, stage, stage_y, v1, pack, rim, edge, band1, band2, h_acc, v2, base, strips,
     lsem, a_s, a_r, t_s, t_r, m_s, m_r, y_s, y_r, c_sem, h_s, h_r, d_sem,
 ):
     gx = lax.axis_index("gx")
@@ -146,17 +146,11 @@
 
     barrier = pltpu.get_barrier_semaphore()
 
-    def greet_row(i, _):
-        pl.semaphore_signal(barrier, inc=1, device_id=(gx, (me + i) % NY), device_id_type=MESH)
-        return 0
-
-    def greet_next(i, _):
-        pl.semaphore_signal(barrier, inc=1, device_id=(up, i), device_id_type=MESH)
-        pl.semaphore_signal(barrier, inc=1, device_id=(down, i), device_id_type=MESH)
-        return 0
-
-    lax.fori_loop(1, NY, greet_row, 0)
-    lax.fori_loop(0, NY, greet_next, 0)
+    for offset in OTHERS + [(0, 0)]:
+        col = shifted(me, offset)
+        for row in (up, down, gx):
+            if row is not gx or offset != (0, 0):
+                pl.semaphore_signal(barrier, inc=1, device_id=(row, col), device_id_type=MESH)
 
     for load in early[:3]:
         load.wait()
@@ -572,6 +566,10 @@
         if g == 0:
             place(0, j, yr[q, 0].astype(jnp.float32))
         place(1 + g, j, acc[q, 0, 0] + yr[q, 1].astype(jnp.float32))
+    for n in range(16):
+        rows_of = pl.ds(n % 4, OUT, stride=ROWS)
+        row = jnp.concatenate([stage[n // 4, j, rows_of, :] for j in range(TXD)], axis=1)
+        base[n] = row.astype(jnp.bfloat16).astype(jnp.float32)
     rims = whole(pack, rim, pl.ds(0, 2), h_s.at[1], h_r.at[1])
     edges[0].wait_recv()
     rims.wait_recv()
@@ -629,9 +627,6 @@
     def band_one(dx, rows):
         return band1[dx, rows, :]
 
-    def band_two(dx, rows):
-        return band2[dx, rows, :]
-
     def column(ref):
         eye = lax.broadcasted_iota(jnp.int32, (OUT, OUT), 0) == lax.broadcasted_iota(jnp.int32, (OUT, OUT), 1)
         return jnp.sum(jnp.where(eye, ref[...], 0.0), axis=1, keepdims=True)
@@ -663,29 +658,20 @@
         h = pre * lax.logistic(pre)
         h = jnp.where(cut, 0.0, h)
         if n == 0:
-            v2_top[...] = jnp.where(gx > 0, h, 0.0).astype(jnp.bfloat16)
+            h = jnp.where(gx > 0, h, 0.0)
         elif n == 17:
-            v2_low[...] = jnp.where(gx < NX - 1, h, 0.0).astype(jnp.bfloat16)
-        else:
-            v2[(n - 1) // 4, pl.ds((n - 1) % 4 * OUT, OUT), :] = h.astype(jnp.bfloat16)
-
-    o_acc[0] = product(lambda dx, rows: w2[dx], every, v2_top[...])[:, : TXD * COLS]
-    for blk in range(TYD):
-        s = product(band_two, every, v2[blk])[:, : TXD * COLS]
-        y = 4 * blk - 1
-        for n in range(6):
-            piece = s[n * OUT : (n + 1) * OUT]
-            if 0 <= y + n < 16:
-                o_acc[y + n] = piece + o_acc[y + n] if n < 2 else piece
-    tail = product(lambda dx, rows: w2[6 + dx], every, v2_low[...])[:, : TXD * COLS]
+            h = jnp.where(gx < NX - 1, h, 0.0)
+        v2[n] = h.astype(jnp.bfloat16)
+
     bias_two = column(b2)
-    for n in range(16):
-        rows = pl.ds(n % 4, OUT, stride=ROWS)
-        base = jnp.concatenate([stage[n // 4, j, rows, :] for j in range(TXD)], axis=1)
-        value = o_acc[n] + bias_two + base.astype(jnp.bfloat16).astype(jnp.float32)
-        if n == 15:
-            value = value + tail
-        shaded[n] = value.astype(jnp.bfloat16)
+
+    def shade(g):
+        row = inv[g]
+        field = jnp.concatenate([v2[row], v2[row + 1], v2[row + 2]], axis=0)
+        z = jnp.dot(band2[...], field, preferred_element_type=jnp.float32)
+        total = z[OUT : 2 * OUT] + pltpu.roll(z[:OUT], 1, 1)
+        total = total + pltpu.roll(z[2 * OUT :], WIDE - 1, 1)
+        return (total[:, : TXD * COLS] + bias_two + base[row]).astype(jnp.bfloat16)
 
     def window(col):
         start = pl.multiple_of(col * (TXD * COLS), TXD * COLS)
@@ -701,12 +687,14 @@
             device_id_type=MESH,
         )
 
-    for offset in OTHERS:
-        g = shifted(me, offset)
-        strips[g] = shaded[inv[g]]
-        strip_copy(g).start()
+    for n in range(0, len(OTHERS), GROUP):
+        columns = [shifted(me, offset) for offset in OTHERS[n : n + GROUP]]
+        for g in columns:
+            strips[g] = shade(g)
+        for g in columns:
+            strip_copy(g).start()
     start = pl.multiple_of(me * (TXD * COLS), TXD * COLS)
-    shown[:, pl.ds(start, TXD * COLS)] = shaded[inv[me]]
+    shown[:, pl.ds(start, TXD * COLS)] = shade(me)
 
     edges[0].wait_send()
     rims.wait_send()
@@ -722,7 +710,7 @@
     parts = pl.ds(0, NY - 1)
     all_strips = pltpu.make_async_remote_copy(
         src_ref=strips.at[parts],
-        dst_ref=shaded.at[parts],
+        dst_ref=strips.at[parts],
         send_sem=d_sem.at[0],
         recv_sem=d_sem.at[1],
         device_id=(gx, right),
@@ -733,24 +721,26 @@
 
 
 def spread_weights(w1, w2, band1, band2):
-    for ref, band, ins, wide, step in ((w1, band1, CH + 1, DEEP1, 4), (w2, band2, OUT, DEEP2, 1)):
+    def pick(ins, wide, first, step):
         chan = lax.broadcasted_iota(jnp.int32, (ins, wide), 0)
         spot = lax.broadcasted_iota(jnp.int32, (ins, wide), 1)
-        pick = []
-        for r in range(ROWS):
-            where = chan * ROWS + r if step == 4 else chan + OUT * r
-            pick.append(jnp.where(spot == where, 1.0, 0.0).astype(jnp.bfloat16))
-        for dx in range(3):
-            for n in range(6):
-                total = None
-                for dy in range(3):
-                    r = n - 1 + dy - 1
-                    if 0 <= r < ROWS:
-                        term = jnp.dot(
-                            ref[3 * dy + dx], pick[r], preferred_element_type=jnp.float32
-                        )
-                        total = term if total is None else total + term
-                band[dx, pl.ds(n * OUT, OUT), :] = total.astype(jnp.bfloat16)
+        return jnp.where(spot == chan * step + first, 1.0, 0.0).astype(jnp.bfloat16)
+
+    def spread(terms):
+        total = None
+        for taps, place in terms:
+            term = jnp.dot(taps, place, preferred_element_type=jnp.float32)
+            total = term if total is None else total + term
+        return total.astype(jnp.bfloat16)
+
+    picks = [pick(CH + 1, DEEP1, r, ROWS) for r in range(ROWS)]
+    for dx in range(3):
+        for n in range(6):
+            rows = [(dy, n + dy - 2) for dy in range(3) if 0 <= n + dy - 2 < ROWS]
+            band1[dx, pl.ds(n * OUT, OUT), :] = spread([(w1[3 * dy + dx], picks[r]) for dy, r in rows])
+    picks = [pick(OUT, 3 * OUT, dy * OUT, 1) for dy in range(3)]
+    for dx in range(3):
+        band2[pl.ds(dx * OUT, OUT), :] = spread([(w2[3 * dy + dx], picks[dy]) for dy in range(3)])
 
 
 def frame(*operands):
@@ -806,13 +796,10 @@
             vmem((2, 2, 32, COLS), f32),
             vmem((TYD + 2, DEEP1, COLS), f32),
             vmem((3, 6 * OUT, DEEP1), bf16),
-            vmem((3, 6 * OUT, DEEP2), bf16),
+            vmem((3 * OUT, 3 * OUT), bf16),
             vmem((18, OUT, WIDE), f32),
-            vmem((TYD, DEEP2, WIDE), bf16),
-            vmem((OUT, WIDE), bf16),
-            vmem((OUT, WIDE), bf16),
+            vmem((18, OUT, WIDE), bf16),
             vmem((16, OUT, TXD * COLS), f32),
-            vmem((16, OUT, TXD * COLS), bf16),
             vmem((NY, OUT, TXD * COLS), bf16),
             dma(()),
             dma((2,)),

time: 57.5 us -> 57.3 us (level)
  no operation moved by 1% of the time
where the time goes in v9:
time: 57.3 us; the launch traced here: 57.2 us
  Pallas kernels  56.5 us (99%)
  local copies, waits for them, and re-layouts  0.71 us (1%)
    pallas_call x1, Pallas kernels, frame(): pl.pallas_call(frame_kernel, name='frame', out_shape=vmem((OUT, NY * TXD...  56.5 us

profile of v9, /device:TPU:0, one launch (start us, length us, event | category | flops | bytes accessed | tf_op | source)
XLA Modules:
  0.0 57.2 jit_solution(16902659523017092812)
XLA Ops:
  0.0 56.5 %frame.1 = bf16[32,4096]{1,0:T(8,128)(2,1)S(1)} custom-call(bf16[128,35,4,128]{3,2,1,0:T(4,128)(2,1)} %bitcast.5, bf16[128,4,128]{2,1,0:T(4,128)(2,1)} %opa_h.1, s32[8,128]{1,0:T(8,128)} %constant.2.clone.rows_h, s32[128,128]{1,0:T(8,128)} %foot_h.1, s32[8,16]{1,0:T(8,128)} %order_h.1, s32[16]{0:T(128)} %panel_h.1, bf16[9,32,36]{2,1,0:T(8,128)(2,1)} %w1_h.1, ...), custom_call_target="tpu_custom_call" | custom-call | tf_op jit(solution)/shard_map/frame/pallas_call | solution.py:751
  56.5 0.7 %copy.12 = bf16[1,1,1,32,4096]{4,3,2,1,0:T(8,128)(2,1)} copy(bf16[1,1,1,32,4096]{4,3,2,1,0:T(8,128)(2,1)S(1)} %bitcast.4) | data formatting | bytes 524288

commit v10 on v9

--- a/solution.py
+++ b/solution.py
@@ -218,7 +218,7 @@
         )
 
     raw = [[raw_copy(q, n) for n in range(4)] for q in range(4)]
-    for n in range(2):
+    for n in range(1):
         for q in range(4):
             raw[q][n].start()
     for q in range(4):
@@ -349,7 +349,7 @@
         device_id=(gx, right),
         device_id_type=MESH,
     )
-    for n in range(2, 4):
+    for n in range(1, 4):
         for q in range(4):
             raw[q][n].start()
 

time: 57.3 us -> 56.7 us (0.990)
  Pallas kernels: 56.5 us -> 55.8 us
    pallas_call x1, Pallas kernels: 56.5 us -> 55.8 us  [frame(): pl.pallas_call(frame_kernel, name='frame', out_shape=vmem((OUT, NY * TXD...]
where the time goes in v10:
time: 56.7 us; the launch traced here: 56.5 us
  Pallas kernels  55.8 us (98%)
  local copies, waits for them, and re-layouts  0.71 us (1%)
    pallas_call x1, Pallas kernels, frame(): pl.pallas_call(frame_kernel, name='frame', out_shape=vmem((OUT, NY * TXD...  55.8 us

profile of v10, /device:TPU:0, one launch (start us, length us, event | category | flops | bytes accessed | tf_op | source)
XLA Modules:
  0.0 56.5 jit_solution(14036087049464229760)
XLA Ops:
  0.0 55.8 %frame.1 = bf16[32,4096]{1,0:T(8,128)(2,1)S(1)} custom-call(bf16[128,35,4,128]{3,2,1,0:T(4,128)(2,1)} %bitcast.5, bf16[128,4,128]{2,1,0:T(4,128)(2,1)} %opa_h.1, s32[8,128]{1,0:T(8,128)} %constant.2.clone.rows_h, s32[128,128]{1,0:T(8,128)} %foot_h.1, s32[8,16]{1,0:T(8,128)} %order_h.1, s32[16]{0:T(128)} %panel_h.1, bf16[9,32,36]{2,1,0:T(8,128)(2,1)} %w1_h.1, ...), custom_call_target="tpu_custom_call" | custom-call | tf_op jit(solution)/shard_map/frame/pallas_call | solution.py:751
  55.8 0.7 %copy.12 = bf16[1,1,1,32,4096]{4,3,2,1,0:T(8,128)(2,1)} copy(bf16[1,1,1,32,4096]{4,3,2,1,0:T(8,128)(2,1)S(1)} %bitcast.4) | data formatting | bytes 524288
